TPU v7x, 32 devices: a whole 2x2x4 slice. The times are simulated.
32 devices in a mesh: space: 2 (over core), energy: 8 (over z, y), mom: 2 (over x).
Axes of the slice: x: 2, y: 2, z: 4, core: 2. Of those that a mesh axis runs over, the one named last changes fastest.
Arguments:
- hamiltonian: float32 [2, 256, 256], P('space'), may hold values from -0.375 to 0.375
- coupling: float32 [2, 224, 224], P('space'), may hold values from -0.75 to 0.75
- self_energy: float32 [2, 8, 4, 2, 256, 256], P('space', 'energy', 'mom'), may hold values from -0.375 to 0.375
- pattern: int32 [2, 256, 256], P('space', 'energy'), may hold values 0 or 1
- momentum_table: int32 [4, 4], replicated, may hold values from 0 to 3
- momentum_weights: float32 [4], replicated, may hold values from 0.2 to 1
- mode_strengths: float32 [2], replicated, may hold values from 0.3 to 1
- mode_offsets: int32 [2], replicated, may hold values from 1 to 5
Outputs:
- new_self_energy: float32 [2, 8, 4, 2, 256, 256], P('space', 'energy', 'mom')
Inputs may be any that keep to these rules, and one draw needn't show every extreme that they name: `momentum_table`: entry [k, q] is the momentum index whose Green's function reaches momentum k through transfer q.
All inputs are finite; a program needn't handle non-finite values. No bound on the sum of `pattern` on one device may be relied on, other than what follows from the above.
Results may differ from a plain program's by a relative error of at most 0.0001.
Values sent between devices are 32-bit elements; how exact they have to be, the bound alone decides.
No kernel may reach another device: no remote copies, remote signals or barrier semaphores. Data moves between devices by JAX's collectives and lax.ppermute only.
A program may use at most 128 MiB of HBM per device.

v0:
```python
import jax
import jax.numpy as jnp
from jax import lax
from jax.sharding import PartitionSpec as P

broadening = 1.0
contact = 1.0
dispersion = 1.0


def from_behind(shard, axis, by):
    count = lax.axis_size(axis)
    pairs = [(i, i + by) for i in range(count) if 0 <= i + by < count]
    return lax.ppermute(shard, axis, pairs)


def matmul_highest(left_side, right_side):
    return jnp.einsum("...ij,...jk->...ik", left_side, right_side, precision=lax.Precision.HIGHEST)


def product_complex(left_side, right_side):
    left_real = left_side[..., 0, :, :]
    left_imag = left_side[..., 1, :, :]
    right_real = right_side[..., 0, :, :]
    right_imag = right_side[..., 1, :, :]
    real_part = matmul_highest(left_real, right_real) - matmul_highest(left_imag, right_imag)
    imag_part = matmul_highest(left_real, right_imag) + matmul_highest(left_imag, right_real)
    return jnp.stack([real_part, imag_part], axis=-3)


def approximate_inverse(matrix):
    order_size = matrix.shape[-1]
    identity = jnp.eye(order_size, dtype=jnp.float32)
    real_part = matrix[..., 0, :, :]
    imag_part = matrix[..., 1, :, :]
    diag_real = jnp.diagonal(real_part, axis1=-2, axis2=-1)
    diag_imag = jnp.diagonal(imag_part, axis1=-2, axis2=-1)
    modulus = diag_real * diag_real + diag_imag * diag_imag
    inverse_real = diag_real / modulus
    inverse_imag = -diag_imag / modulus
    outside = 1.0 - identity
    off_real = real_part * outside
    off_imag = imag_part * outside
    row_real = inverse_real[..., :, None]
    row_imag = inverse_imag[..., :, None]
    scaled = jnp.stack(
        [row_real * off_real - row_imag * off_imag, row_real * off_imag + row_imag * off_real],
        axis=-3,
    )
    series = product_complex(scaled, scaled) - scaled
    series_real = series[..., 0, :, :] + identity
    series_imag = series[..., 1, :, :]
    column_real = inverse_real[..., None, :]
    column_imag = inverse_imag[..., None, :]
    return jnp.stack(
        [
            series_real * column_real - series_imag * column_imag,
            series_real * column_imag + series_imag * column_real,
        ],
        axis=-3,
    )


def build_system(
    hamiltonian_slice, self_slice, energy_index, momentum_index, energies_all, momenta_all
):
    order_size = hamiltonian_slice.shape[-1]
    identity = jnp.eye(order_size, dtype=jnp.float32)
    symmetric = 0.5 * (hamiltonian_slice + hamiltonian_slice.T)
    energy = -2.0 + 4.0 * energy_index.astype(jnp.float32) / energies_all
    kinetic = dispersion * (
        1.0 - jnp.cos(2.0 * jnp.pi * momentum_index.astype(jnp.float32) / momenta_all)
    )
    diagonal_shift = energy[:, None] - kinetic[None, :]
    real_part = diagonal_shift[:, :, None, None] * identity - symmetric - self_slice[:, :, 0]
    imag_part = broadening * identity - self_slice[:, :, 1]
    return jnp.stack([real_part, imag_part], axis=2)


def contact_term(surface):
    return jnp.stack(
        [jnp.zeros((surface, surface), jnp.float32), -contact * jnp.eye(surface, dtype=jnp.float32)]
    )


def embed_first(matrix, term):
    width = term.shape[-1]
    return matrix.at[..., :width, :width].add(-term)


def embed_last(matrix, term):
    width = term.shape[-1]
    order_size = matrix.shape[-1]
    return matrix.at[..., order_size - width :, order_size - width :].add(-term)


def sandwich(coupling_block, middle):
    return jnp.einsum(
        "ji,...jk,kl->...il",
        coupling_block,
        middle,
        coupling_block,
        precision=lax.Precision.HIGHEST,
    )


def sandwich_back(coupling_block, middle):
    return jnp.einsum(
        "ij,...jk,lk->...il",
        coupling_block,
        middle,
        coupling_block,
        precision=lax.Precision.HIGHEST,
    )


def convolve_energy(green_rows, mode_strengths, mode_offsets):
    point_count = green_rows.shape[0]
    widths = [(point_count, point_count)] + [(0, 0)] * (green_rows.ndim - 1)
    padded = jnp.pad(green_rows, widths)
    accumulated = jnp.zeros_like(green_rows)
    for mode_index in range(mode_strengths.shape[0]):
        offset_now = mode_offsets[mode_index]
        below_part = lax.dynamic_slice_in_dim(padded, point_count - offset_now, point_count, 0)
        above_part = lax.dynamic_slice_in_dim(padded, point_count + offset_now, point_count, 0)
        accumulated = accumulated + mode_strengths[mode_index] * (below_part + above_part)
    return accumulated


def momentum_coefficients(momentum_table, momentum_weights):
    momentum_count = momentum_table.shape[0]
    labels = jnp.arange(momentum_count, dtype=jnp.int32)
    matches = (momentum_table[:, :, None] == labels[None, None, :]).astype(jnp.float32)
    return jnp.einsum("q,kqj->kj", momentum_weights, matches, precision=lax.Precision.HIGHEST)


def keep_state(held_terms, message):
    return (held_terms, message)


def body(
    hamiltonian,
    coupling,
    self_energy,
    pattern,
    momentum_table,
    momentum_weights,
    mode_strengths,
    mode_offsets,
):
    orbitals = hamiltonian.shape[-1]
    surface = coupling.shape[-1]
    energies_here = self_energy.shape[1]
    momenta_here = self_energy.shape[2]
    energy_groups = lax.axis_size("energy")
    momentum_groups = lax.axis_size("mom")
    slices = lax.axis_size("space")
    position = lax.axis_index("space")
    energies_all = energies_here * energy_groups
    momenta_all = momenta_here * momentum_groups
    energy_index = lax.axis_index("energy") * energies_here + jnp.arange(
        energies_here, dtype=jnp.int32
    )
    momentum_index = lax.axis_index("mom") * momenta_here + jnp.arange(
        momenta_here, dtype=jnp.int32
    )
    item_count = energies_here * momenta_here
    system = build_system(
        hamiltonian[0], self_energy[0], energy_index, momentum_index, energies_all, momenta_all
    )
    system = system.reshape(item_count, 2, orbitals, orbitals)
    coupling_block = coupling[0]
    corner = orbitals - surface
    first_slice = position == 0
    last_slice = position == slices - 1
    zero_terms = jnp.zeros((item_count, 2, surface, surface), jnp.float32)
    single_source = contact_term(surface)
    zero_message = jnp.zeros((2, surface, surface), jnp.float32)

    def forward_turn(sweep_step, carry):
        received = from_behind(carry[1], "space", 1)
        item_now = sweep_step - position

        def forward_active(held_terms, message):
            incoming = jnp.where(first_slice, single_source, received)
            current = lax.dynamic_index_in_dim(system, item_now, 0, keepdims=False)
            green_left = approximate_inverse(embed_first(current, incoming))
            stored = lax.dynamic_update_index_in_dim(held_terms, incoming, item_now, 0)
            return (stored, sandwich(coupling_block, green_left[..., corner:, corner:]))

        return lax.cond(
            (item_now >= 0) & (item_now < item_count),
            forward_active,
            keep_state,
            carry[0],
            carry[1],
        )

    def backward_turn(sweep_step, carry):
        received = from_behind(carry[1], "space", -1)
        item_now = sweep_step - (slices - 1 - position)

        def backward_active(held_terms, message):
            incoming = jnp.where(last_slice, single_source, received)
            right_now = sandwich_back(coupling_block, incoming)
            current = lax.dynamic_index_in_dim(system, item_now, 0, keepdims=False)
            green_right = approximate_inverse(embed_last(current, right_now))
            stored = lax.dynamic_update_index_in_dim(held_terms, right_now, item_now, 0)
            return (stored, green_right[..., :surface, :surface])

        return lax.cond(
            (item_now >= 0) & (item_now < item_count),
            backward_active,
            keep_state,
            carry[0],
            carry[1],
        )

    turn_total = slices + item_count - 1
    left_terms, unused_left = lax.fori_loop(0, turn_total, forward_turn, (zero_terms, zero_message))
    right_terms, unused_right = lax.fori_loop(
        0, turn_total, backward_turn, (zero_terms, zero_message)
    )
    green_final = approximate_inverse(embed_last(embed_first(system, left_terms), right_terms))
    coefficients = momentum_coefficients(momentum_table, momentum_weights)
    mask_rows = pattern[0].astype(jnp.float32)
    row_count = orbitals // energy_groups
    blocks = green_final.reshape(energies_here, momenta_here, 2, energy_groups, row_count, orbitals)
    regrouped = lax.all_to_all(blocks, "energy", split_axis=3, concat_axis=0, tiled=True)
    regrouped = regrouped.reshape(energies_all, momenta_here, 2, row_count, orbitals)
    phonon = convolve_energy(regrouped, mode_strengths, mode_offsets)
    own_rows = lax.dynamic_slice_in_dim(
        coefficients, lax.axis_index("mom") * momenta_here, momenta_here, 0
    )
    mixed_terms = jnp.zeros_like(phonon) + jnp.einsum(
        "kj,ej...->ek...",
        own_rows,
        lax.all_gather(phonon, "mom", axis=1, tiled=True),
        precision=lax.Precision.HIGHEST,
    )
    mixed_terms = mixed_terms * mask_rows
    mixed_terms = mixed_terms.reshape(energies_all, momenta_here, 2, 1, row_count, orbitals)
    returned = lax.all_to_all(mixed_terms, "energy", split_axis=0, concat_axis=3, tiled=True)
    return returned.reshape(1, energies_here, momenta_here, 2, orbitals, orbitals)


def solution(mesh):
    return jax.shard_map(
        body,
        mesh=mesh,
        in_specs=(
            P("space", None, None),
            P("space", None, None),
            P("space", "energy", "mom", None, None, None),
            P("space", "energy", None),
            P(),
            P(),
            P(),
            P(),
        ),
        out_specs=P("space", "energy", "mom", None, None, None),
        check_vma=False,
    )
```

profile of v0, /device:TPU:0, one launch (start us, length us, event | category | flops | bytes accessed | tf_op | source)
XLA Modules:
  0.0 275.0 jit_solution(17039815926781231370)
XLA Ops:
  7.3 1.3 copy.108
  15.1 32.7 %while.36 = (s32[]{:T(128)}, f32[2,2,224,224]{3,2,1,0:T(8,128)}, f32[2,224,224]{2,1,0:T(8,128)S(1)}, s32[]{:T(128)}, pred[]{:T(512)}, /*index=5*/f32[2,224,224]{...) while((s32[]{:T(128)}, f32[2,2,224,224]{3,2,1,0:T(8,128)}, ...), condition=%wide.region_3.0_spmd, body=%wide.region_0.3_spmd.sunk | while | flops 1347138048 | bytes 16336718 | solution.py:220
  15.1 2.4 collective-permute-start
  17.6 1.4 collective-permute-done
  19.0 11.2 %conditional.4 = ((f32[2,2,224,224]{3,2,1,0:T(8,128)}, f32[2,224,224]{2,1,0:T(8,128)S(1)})) conditional(s32[]{:T(128)} %convert_element_type.173, (f32[2,2,224,224]{3,2,1,0:T(8,128)}, f32[2,224,224]{2,1,0:T(8,128)S(1)}) %tuple.116, (pred[]{:T(512)}, f32[2,224,224]{2,1,0:T(8,128)S(1)}, f32[2,224,224]{2,1,0:T(8,128)S(1)}, s32[]{:T(128)}, ...), branch_computations={%region_1.0_spmd, %region_2.2_spmd} | conditional | flops 1347138048 | bytes 14730827 | solution.py:191
  19.1 2.3 scatter-add.0
  21.5 2.3 gather_fusion
  23.8 2.3 gather_fusion.1
  30.2 1.3 collective-permute-start
  31.5 1.4 collective-permute-done
  32.9 11.3 %conditional.4 = ((f32[2,2,224,224]{3,2,1,0:T(8,128)}, f32[2,224,224]{2,1,0:T(8,128)S(1)})) conditional(s32[]{:T(128)} %convert_element_type.173, (f32[2,2,224,224]{3,2,1,0:T(8,128)}, f32[2,224,224]{2,1,0:T(8,128)S(1)}) %tuple.116, (pred[]{:T(512)}, f32[2,224,224]{2,1,0:T(8,128)S(1)}, f32[2,224,224]{2,1,0:T(8,128)S(1)}, s32[]{:T(128)}, ...), branch_computations={%region_1.0_spmd, %region_2.2_spmd} | conditional | flops 1347138048 | bytes 14730827 | solution.py:191
  33.1 2.3 scatter-add.0
  35.4 2.3 gather_fusion
  37.8 2.3 gather_fusion.1
  44.2 2.3 collective-permute-start
  46.5 1.4 collective-permute-done
  47.9 1.6 fusion.55
  49.4 5.2 %scatter-add.16 = f32[2,2,256,256]{3,2,0,1:T(8,128)} dynamic-update-slice(f32[2,2,256,256]{3,2,0,1:T(8,128)} %copy-done.2, f32[2,2,224,224]{3,2,0,1:T(8,128)S(1)} %fusion.55, s32[]{:T(128)} %constant.266.clone.1, s32[]{:T(128)} %constant.266.clone.1, s32[]{:T(128)} %constant.266.clone.1, s32[]{:T(128)} %constant.266.clone.1) | dynamic-update-slice | bytes 1605636 | tf_op jit(solution)/shard_map/scatter-add | solution.py:88
  55.7 61.7 %while.37 = (s32[]{:T(128)}, f32[2,2,224,224]{3,2,1,0:T(8,128)}, f32[2,224,224]{2,1,0:T(8,128)S(1)}, s32[]{:T(128)}, pred[]{:T(512)}, /*index=5*/f32[2,224,224]{...) while((s32[]{:T(128)}, f32[2,2,224,224]{3,2,1,0:T(8,128)}, ...), condition=%wide.region_7.8_spmd, body=%wide.region_4.7_spmd.sunk | while | flops 1347037696 | bytes 17139036 | solution.py:221
  55.9 1.4 collective-permute-start.1
  57.4 13.1 %collective-permute-done.1 = f32[2,224,224]{1,2,0:T(8,128)} collective-permute-done((f32[2,224,224]{1,2,0:T(8,128)S(1)}, f32[2,224,224]{1,2,0:T(8,128)}, u32[]{:S(2)}, u32[]{:S(2)}) %collective-permute-start.1) | collective-permute-done | bytes 401440 | tf_op jit(solution)/shard_map/while/body/eval_jaxpr/ppermute | solution.py:14
  72.0 14.8 %collective-permute-done.1 = f32[2,224,224]{1,2,0:T(8,128)} collective-permute-done((f32[2,224,224]{1,2,0:T(8,128)S(1)}, f32[2,224,224]{1,2,0:T(8,128)}, u32[]{:S(2)}, u32[]{:S(2)}) %collective-permute-start.1) | collective-permute-done | bytes 401440 | tf_op jit(solution)/shard_map/while/body/eval_jaxpr/ppermute | solution.py:14
  86.8 13.3 %conditional.5 = ((f32[2,2,224,224]{3,2,1,0:T(8,128)}, f32[2,224,224]{2,1,0:T(8,128)S(1)})) conditional(s32[]{:T(128)} %convert_element_type.174, (f32[2,2,224,224]{3,2,1,0:T(8,128)}, f32[2,224,224]{2,1,0:T(8,128)S(1)}) %tuple.119, (pred[]{:T(512)}, f32[2,224,224]{1,2,0:T(8,128)}, f32[2,224,224]{1,2,0:T(8,128)}, f32[224,224]{1,0:T(8,128)S(1)}, ...), branch_computations={%region_5.5_spmd, %region_6.6_spmd} | conditional | flops 1347037696 | bytes 14730331 | solution.py:211
  86.8 1.6 fusion.23
  88.4 1.3 bitcast_dynamic-update-slice_fusion.1
  90.0 3.4 %scatter-add.10 = f32[2,256,256]{2,1,0:T(8,128)S(1)} dynamic-update-slice(f32[2,256,256]{2,1,0:T(8,128)S(1)} %dynamic-slice_bitcast_fusion.2, f32[2,224,224]{2,1,0:T(8,128)S(1)} %fusion.22, s32[]{:T(128)} %constant.251.clone, s32[]{:T(128)} %constant.253.clone, s32[]{:T(128)} %constant.253.clone) | dynamic-update-slice | bytes 802820 | tf_op jit(solution)/shard_map/while/body/eval_jaxpr/cond/branch_1_fun/scatter-add | solution.py:94
  93.4 2.3 gather_fusion.2
  95.8 2.3 gather_fusion.3
  101.6 2.5 collective-permute-done.1
  104.1 13.3 %conditional.5 = ((f32[2,2,224,224]{3,2,1,0:T(8,128)}, f32[2,224,224]{2,1,0:T(8,128)S(1)})) conditional(s32[]{:T(128)} %convert_element_type.174, (f32[2,2,224,224]{3,2,1,0:T(8,128)}, f32[2,224,224]{2,1,0:T(8,128)S(1)}) %tuple.119, (pred[]{:T(512)}, f32[2,224,224]{1,2,0:T(8,128)}, f32[2,224,224]{1,2,0:T(8,128)}, f32[224,224]{1,0:T(8,128)S(1)}, ...), branch_computations={%region_5.5_spmd, %region_6.6_spmd} | conditional | flops 1347037696 | bytes 14730331 | solution.py:211
  104.1 1.6 fusion.23
  105.7 1.4 bitcast_dynamic-update-slice_fusion.1
  107.3 3.4 %scatter-add.10 = f32[2,256,256]{2,1,0:T(8,128)S(1)} dynamic-update-slice(f32[2,256,256]{2,1,0:T(8,128)S(1)} %dynamic-slice_bitcast_fusion.2, f32[2,224,224]{2,1,0:T(8,128)S(1)} %fusion.22, s32[]{:T(128)} %constant.251.clone, s32[]{:T(128)} %constant.253.clone, s32[]{:T(128)} %constant.253.clone) | dynamic-update-slice | bytes 802820 | tf_op jit(solution)/shard_map/while/body/eval_jaxpr/cond/branch_1_fun/scatter-add | solution.py:94
  110.8 2.3 gather_fusion.2
  113.2 2.3 gather_fusion.3
  117.4 1.5 slice_add_fusion
  118.9 7.0 %scatter-add.17 = f32[2,2,256,256]{3,2,0,1:T(8,128)S(1)} dynamic-update-slice(f32[2,2,256,256]{3,2,0,1:T(8,128)S(1)} %copy-done.3, f32[2,2,224,224]{3,2,0,1:T(8,128)S(1)} %slice_add_fusion, s32[]{:T(128)} %constant.266.clone.1, s32[]{:T(128)} %constant.266.clone.1, s32[]{:T(128)} %constant.271.clone.1, s32[]{:T(128)} %constant.271.clone.1) | dynamic-update-slice | bytes 1605636 | tf_op jit(solution)/shard_map/scatter-add | solution.py:94
  126.1 16.5 %copy.78 = f32[2,256,256]{0,2,1:T(8,128)} copy(f32[2,256,256]{2,1,0:T(8,128)S(1)} %get-tuple-element.573) | data formatting | bytes 1048576 | tf_op jit(solution)/shard_map/squeeze | solution.py:34
  142.5 2.3 gather_fusion.4
  145.0 16.4 %copy.80 = f32[2,256,256]{0,2,1:T(8,128)} copy(f32[2,256,256]{2,1,0:T(8,128)S(1)} %get-tuple-element.574) | data formatting | bytes 1048576 | tf_op jit(solution)/shard_map/squeeze | solution.py:35
  161.4 2.3 gather_fusion.5
  168.2 1.5 pad_maximum_fusion.4
  169.8 6.6 %all-to-all-start = ((f32[1,2,2,8,32,256]{5,1,4,2,0,3:T(2,128)}), f32[1,2,2,8,32,256]{5,1,4,2,0,3:T(2,128)S(1)}, u32[]{:S(2)}, u32[]{:S(2)}) async-start(f32[1,2,2,8,32,256]{5,1,4,2,0,3:T(2,128)} %pad_maximum_fusion.4), calls=%async_computation | async-start | bytes 2097152 | tf_op jit(solution)/shard_map/all_to_all | solution.py:229
  182.6 10.2 %all-to-all-done = f32[1,2,2,8,32,256]{5,1,4,2,0,3:T(2,128)S(1)} async-done(((f32[1,2,2,8,32,256]{5,1,4,2,0,3:T(2,128)}), f32[1,2,2,8,32,256]{5,1,4,2,0,3:T(2,128)S(1)}, u32[]{:S(2)}, u32[]{:S(2)}) %all-to-all-start) | async-done | bytes 1048608 | tf_op jit(solution)/shard_map/all_to_all | solution.py:229
  192.8 3.7 %multiply_add_fusion.6 = f32[8,2,2,32,256]{4,1,3,2,0:T(2,128)S(1)} fusion(s32[]{:T(128)S(6)} %select_n.58, f32[8,2,2,32,256]{4,1,3,2,0:T(2,128)S(1)} %bitcast.181, s32[]{:T(128)S(6)} %select_n.57, s32[]{:T(128)S(6)} %select_n.56, s32[]{:T(128)S(6)} %select_n.55, f32[]{:T(128)} %bitcast.46, f32[]{:T(128)} %bitcast.22), kind=kLoop, calls=%fused_computation.106 | loop fusion | flops 1310720 | bytes 2097176 | tf_op jit(solution)/shard_map/add | solution.py:126
  197.9 31.6 %all-gather.2.cloned.1.call-done = f32[8,4,2,32,256]{4,3,2,0,1:T(8,128)} async-done(((f32[8,2,2,32,256]{4,3,2,0,1:T(8,128)}), f32[8,4,2,32,256]{4,3,2,0,1:T(8,128)}) %all-gather.2.cloned.1.call-update) | async-done | bytes 2097168 | tf_op jit(solution)/shard_map/all_gather | solution.py:238
  229.5 6.5 %fusion.45 = f32[8,2,2,1,32,256]{5,1,4,2,3,0:T(2,128)S(1)} fusion(f32[8,4,2,32,256]{4,3,2,0,1:T(8,128)} %all-gather.2.cloned.1.call-done, f32[32,256]{1,0:T(8,128)S(1)} %convert_bitcast_fusion, f32[4,4]{1,0:T(4,128)S(1)} %bitcast.186, s32[]{:T(128)S(6)} %select_n.59), kind=kOutput, calls=%fused_computation.92 | convolution fusion | flops 12845056 | bytes 3179524 | tf_op jit(solution)/shard_map/kj,ej...->ek.../dot_general | solution.py:235
  236.1 30.9 %all_to_all.30 = f32[8,2,2,1,32,256]{5,1,4,2,3,0:T(2,128)S(1)} all-to-all(f32[8,2,2,1,32,256]{5,1,4,2,3,0:T(2,128)S(1)} %fusion.45), channel_id=1, replica_groups=mesh['space'=2,'energy'=8,'mom'=2] {'energy'}, dimensions={0} | all-to-all | bytes 2097152 | tf_op jit(solution)/shard_map/all_to_all | solution.py:243
  (129 shorter events, 32.3 us)
Async XLA Ops:
  6.5 191.1 %copy-start = (f32[4]{0:T(128)S(1)}, f32[4]{0:T(128)}, u32[]{:S(2)}) copy-start(f32[4]{0:T(128)} %param.29) | copy-start | bytes 52
  6.5 3.2 %copy-start.9 = (f32[1,256,256]{2,1,0:T(8,128)S(1)}, f32[1,256,256]{2,1,0:T(8,128)}, u32[]{:S(2)}) copy-start(f32[1,256,256]{2,1,0:T(8,128)} %param.24) | copy-start | bytes 786436
  6.6 3.4 %copy-start.7 = (f32[256,256]{1,0:T(8,128)}, f32[256,256]{1,0:T(8,128)S(1)}, u32[]{:S(2)}) copy-start(f32[256,256]{1,0:T(8,128)S(1)} %fusion.57) | copy-start | bytes 786436
  10.0 0.8 copy-start.4
  10.0 1.0 copy-start.5
  11.0 4.1 %copy-start.1 = (f32[1,224,224]{2,1,0:T(8,128)S(1)}, f32[1,224,224]{2,1,0:T(8,128)}, u32[]{:S(2)}) copy-start(f32[1,224,224]{2,1,0:T(8,128)} %param.25) | copy-start | bytes 602116
  11.1 1.0 copy-start.2
  15.1 3.8 %collective-permute-start = (f32[2,224,224]{2,1,0:T(8,128)S(1)}, f32[2,224,224]{2,1,0:T(8,128)S(1)}, u32[]{:S(2)}, u32[]{:S(2)}) collective-permute-start(f32[2,224,224]{2,1,0:T(8,128)S(1)} %get-tuple-element.708), channel_id=1, source_target_pairs={{0,16},{1,17},{2,18},{3,19},{4,20},{5,21},{6,22},{7,23},{8,24},{9,... | collective-permute-start | bytes 1204232 | tf_op jit(solution)/shard_map/while/body/eval_jaxpr/ppermute | solution.py:14
  30.2 2.7 collective-permute-start
  44.2 3.7 %collective-permute-start = (f32[2,224,224]{2,1,0:T(8,128)S(1)}, f32[2,224,224]{2,1,0:T(8,128)S(1)}, u32[]{:S(2)}, u32[]{:S(2)}) collective-permute-start(f32[2,224,224]{2,1,0:T(8,128)S(1)} %get-tuple-element.708), channel_id=1, source_target_pairs={{0,16},{1,17},{2,18},{3,19},{4,20},{5,21},{6,22},{7,23},{8,24},{9,... | collective-permute-start | bytes 1204232 | tf_op jit(solution)/shard_map/while/body/eval_jaxpr/ppermute | solution.py:14
  55.7 61.7 %copy-start.3 = (f32[2,2,256,256]{3,2,0,1:T(8,128)S(1)}, f32[2,2,256,256]{3,2,0,1:T(8,128)}, u32[]{:S(2)}) copy-start(f32[2,2,256,256]{3,2,0,1:T(8,128)} %scatter-add.16) | copy-start | bytes 3145732
  55.9 14.5 %collective-permute-start.1 = (f32[2,224,224]{1,2,0:T(8,128)S(1)}, f32[2,224,224]{1,2,0:T(8,128)}, u32[]{:S(2)}, u32[]{:S(2)}) collective-permute-start(f32[2,224,224]{1,2,0:T(8,128)S(1)} %copy.110), channel_id=1, source_target_pairs={{16,0},{17,1},{18,2},{19,3},{20,4},{21,5},{22,6},{23,7},{24,8},{25... | collective-permute-start | bytes 1204232 | tf_op jit(solution)/shard_map/while/body/eval_jaxpr/ppermute | solution.py:14
  70.6 16.1 %collective-permute-start.1 = (f32[2,224,224]{1,2,0:T(8,128)S(1)}, f32[2,224,224]{1,2,0:T(8,128)}, u32[]{:S(2)}, u32[]{:S(2)}) collective-permute-start(f32[2,224,224]{1,2,0:T(8,128)S(1)} %copy.110), channel_id=1, source_target_pairs={{16,0},{17,1},{18,2},{19,3},{20,4},{21,5},{22,6},{23,7},{24,8},{25... | collective-permute-start | bytes 1204232 | tf_op jit(solution)/shard_map/while/body/eval_jaxpr/ppermute | solution.py:14
  100.3 3.8 %collective-permute-start.1 = (f32[2,224,224]{1,2,0:T(8,128)S(1)}, f32[2,224,224]{1,2,0:T(8,128)}, u32[]{:S(2)}, u32[]{:S(2)}) collective-permute-start(f32[2,224,224]{1,2,0:T(8,128)S(1)} %copy.110), channel_id=1, source_target_pairs={{16,0},{17,1},{18,2},{19,3},{20,4},{21,5},{22,6},{23,7},{24,8},{25... | collective-permute-start | bytes 1204232 | tf_op jit(solution)/shard_map/while/body/eval_jaxpr/ppermute | solution.py:14
  144.9 18.9 %copy-start.6 = (f32[256,256]{1,0:T(8,128)S(1)}, f32[256,256]{1,0:T(8,128)}, u32[]{:S(2)}) copy-start(f32[256,256]{1,0:T(8,128)} %broadcast_subtract_fusion) | copy-start | bytes 786436
  166.3 1.0 copy-start.8
  167.4 9.3 %copy-start.11 = (s32[2]{0:T(128)S(1)}, s32[2]{0:T(128)}, u32[]{:S(2)}) copy-start(s32[2]{0:T(128)} %param.31) | copy-start | bytes 28
  167.4 14.6 %copy-start.12 = (f32[2]{0:T(128)S(1)}, f32[2]{0:T(128)}, u32[]{:S(2)}) copy-start(f32[2]{0:T(128)} %param.30) | copy-start | bytes 28
  169.8 23.0 %all-to-all-start = ((f32[1,2,2,8,32,256]{5,1,4,2,0,3:T(2,128)}), f32[1,2,2,8,32,256]{5,1,4,2,0,3:T(2,128)S(1)}, u32[]{:S(2)}, u32[]{:S(2)}) async-start(f32[1,2,2,8,32,256]{5,1,4,2,0,3:T(2,128)} %pad_maximum_fusion.4), calls=%async_computation | async-start | bytes 2097152 | tf_op jit(solution)/shard_map/all_to_all | solution.py:229
  176.4 21.3 %copy-start.13 = (s32[4,4]{1,0:T(4,128)S(1)}, s32[4,4]{1,0:T(4,128)}, u32[]{:S(2)}) copy-start(s32[4,4]{1,0:T(4,128)} %param.28) | copy-start | bytes 196
  176.4 21.5 %copy-start.10 = (s32[1,32,256]{2,1,0:T(8,128)S(1)}, s32[1,32,256]{2,1,0:T(8,128)}, u32[]{:S(2)}) copy-start(s32[1,32,256]{2,1,0:T(8,128)} %param.27) | copy-start | bytes 98308
  176.4 53.1 %all-gather.2.cloned.1.call-start = ((), (), s32[]{:S(2)}) async-start(), calls=%async_computation.2 | async-start | bytes 3145728 | tf_op jit(solution)/shard_map/all_gather | solution.py:238
Sparse Core Ops, SparseCore 0:
  197.8 31.6 all-gather.1
where the time goes:
time: 276 us; the launch traced here: 275 us
  local copies, waits for them, and re-layouts  93.8 us (34%)
  waiting for transfers between devices  76.4 us (28%)
  blocking collectives  30.9 us (11%)
  matrix products  24 us (9%)
  between operations  18.5 us (7%)
  starting transfers between devices  16.9 us (6%)
  other arithmetic  13.6 us (5%)
    ppermute x6, waiting for transfers between devices, from_behind(): return lax.ppermute(shard, axis, pairs)  34.6 us
    all_gather x1, waiting for transfers between devices, body(): lax.all_gather(phonon, 'mom', axis=1, tiled=True)  31.6 us
    all_to_all x1, blocking collectives, body(): lax.all_to_all(mixed_terms, 'energy', split_axis=0, concat_axis=3, tiled=...  30.9 us
    squeeze x6, local copies, waits for them, and re-layouts, approximate_inverse(): real_part = matrix[..., 0, :, :]  16.7 us
    squeeze x1, local copies, waits for them, and re-layouts, approximate_inverse(): imag_part = matrix[..., 1, :, :]  16.4 us
    scatter-add x3, local copies, waits for them, and re-layouts, embed_last(): return matrix.at[..., order_size - width:, order_size - width:].add(-term)  13.8 us
    gather x6, local copies, waits for them, and re-layouts, approximate_inverse(): diag_imag = jnp.diagonal(imag_part, axis1=-2, axis2=-1)  11.8 us
    gather x6, local copies, waits for them, and re-layouts, approximate_inverse(): diag_real = jnp.diagonal(real_part, axis1=-2, axis2=-1)  11.8 us
  transfers between devices with their start and end apart: 8, of which 8 were waited for; matrix products, arithmetic and copies ran while one was open for 0% of the time, Pallas kernels for 0%

commit v1 on v0

v1 whole, which is shorter than its diff:
```python
import functools

import jax
import jax.numpy as jnp
from jax import lax
from jax.experimental import pallas as pl
from jax.experimental.pallas import tpu as pltpu
from jax.sharding import PartitionSpec as P

broadening = 1.0
contact = 1.0
dispersion = 1.0
parts = 2
kernel_memory = 24 * 1024 * 1024


def split_pair(value):
    high = value.astype(jnp.bfloat16)
    return high, (value - high.astype(jnp.float32)).astype(jnp.bfloat16)


def product(left_pair, right_pair):
    left_high, left_low = left_pair
    right_high, right_low = right_pair
    dot = functools.partial(jnp.dot, preferred_element_type=jnp.float32)
    return dot(left_high, right_high) + dot(left_high, right_low) + dot(left_low, right_high)


def diagonal_mask(order_size):
    rows = lax.broadcasted_iota(jnp.int32, (order_size, order_size), 0)
    columns = lax.broadcasted_iota(jnp.int32, (order_size, order_size), 1)
    return rows == columns


def inverse_pair(real_part, imag_part):
    order_size = real_part.shape[-1]
    on_diagonal = diagonal_mask(order_size)
    only_real = jnp.where(on_diagonal, real_part, 0.0)
    only_imag = jnp.where(on_diagonal, imag_part, 0.0)

    def reciprocal(axis):
        diag_real = jnp.sum(only_real, axis=axis, keepdims=True)
        diag_imag = jnp.sum(only_imag, axis=axis, keepdims=True)
        modulus = diag_real * diag_real + diag_imag * diag_imag
        return diag_real / modulus, -diag_imag / modulus

    row_real, row_imag = reciprocal(1)
    column_real, column_imag = reciprocal(0)
    off_real = jnp.where(on_diagonal, 0.0, real_part)
    off_imag = jnp.where(on_diagonal, 0.0, imag_part)
    scaled_real = row_real * off_real - row_imag * off_imag
    scaled_imag = row_real * off_imag + row_imag * off_real
    pair_real = split_pair(scaled_real)
    pair_imag = split_pair(scaled_imag)
    pair_both = split_pair(scaled_real + scaled_imag)
    square_real = product(pair_real, pair_real)
    square_imag = product(pair_imag, pair_imag)
    square_both = product(pair_both, pair_both)
    series_real = square_real - square_imag - scaled_real + jnp.where(on_diagonal, 1.0, 0.0)
    series_imag = square_both - square_real - square_imag - scaled_imag
    return (
        series_real * column_real - series_imag * column_imag,
        series_real * column_imag + series_imag * column_real,
    )


def start_kernel(
    surface, slice_ref, shift_ref, hamiltonian_ref, coupling_ref, self_ref, known_ref, face_ref,
    base_ref, term_ref, wide_ref, green_ref,
):
    order_size = hamiltonian_ref.shape[-1]
    corner = order_size - surface
    item = pl.program_id(0)
    slice_now = slice_ref[0]

    @pl.when(item == 0)
    def _():
        base_ref[...] = 0.5 * (hamiltonian_ref[0] + hamiltonian_ref[0].T)

        @pl.when(slice_now == 0)
        def _():
            rows = lax.broadcasted_iota(jnp.int32, (order_size, order_size), 0)
            inside = jnp.logical_and(diagonal_mask(order_size), rows < surface)
            term_ref[...] = jnp.where(inside, contact, 0.0)

        @pl.when(slice_now != 0)
        def _():
            wide_ref[...] = jnp.zeros_like(wide_ref)
            wide_ref[corner:, :surface] = coupling_ref[0]
            wide = wide_ref[...]
            term_ref[...] = contact * product(split_pair(wide), split_pair(wide.T))

    on_diagonal = diagonal_mask(order_size)
    real_part = jnp.where(on_diagonal, shift_ref[item], 0.0) - base_ref[...] - self_ref[0, 0]
    imag_part = jnp.where(on_diagonal, broadening, 0.0) - self_ref[0, 1] + term_ref[...]
    known_ref[0, 0] = real_part
    known_ref[0, 1] = imag_part
    green_real, green_imag = inverse_pair(real_part, imag_part)
    green_ref[0] = green_real
    green_ref[1] = green_imag
    first = pl.multiple_of(jnp.where(slice_now == 0, corner, 0), 8)
    face_ref[0] = green_ref[:, pl.ds(first, surface), :]


def finish_kernel(
    surface, pieces, slice_ref, coupling_ref, known_ref, face_ref, out_ref,
    wide_ref, side_high_ref, side_low_ref, across_high_ref, across_low_ref, face_full_ref,
):
    order_size = known_ref.shape[-1]
    corner = order_size - surface
    item = pl.program_id(0)
    slice_now = slice_ref[0]

    @pl.when(item == 0)
    def _():
        face_full_ref[...] = jnp.zeros_like(face_full_ref)
        wide_ref[...] = jnp.zeros_like(wide_ref)
        wide_ref[corner:, :surface] = coupling_ref[...]
        plain = wide_ref[...]
        turned = plain.T
        at_first = slice_now == 0
        side_high_ref[...], side_low_ref[...] = split_pair(jnp.where(at_first, plain, turned))
        across_high_ref[...], across_low_ref[...] = split_pair(jnp.where(at_first, turned, plain))

    first = pl.multiple_of(jnp.where(slice_now == 0, 0, corner), 8)
    face_full_ref[:, pl.ds(first, surface), :] = face_ref[0]
    side = (side_high_ref[...], side_low_ref[...])
    across = (across_high_ref[...], across_low_ref[...])
    through_real = product(side, split_pair(face_full_ref[0]))
    through_imag = product(side, split_pair(face_full_ref[1]))
    real_part = known_ref[0, 0] - product(split_pair(through_real), across)
    imag_part = known_ref[0, 1] - product(split_pair(through_imag), across)
    green = inverse_pair(real_part, imag_part)
    for piece, segments in enumerate(pieces):
        filled = 0
        for part, row, count in segments:
            out_ref[piece, 0, filled : filled + count, :] = green[part][row : row + count, :]
            filled += count


def scatter_kernel(
    energies_all, momenta_all, energies_here, momenta_here, momentum_groups, branches,
    offset_ref, strength_ref, coefficient_ref, mask_ref, in_ref, out_ref, mixed_ref,
):
    def place(energy, momentum):
        group = (energy // energies_here) * momentum_groups + momentum // momenta_here
        return group, (energy % energies_here) * momenta_here + momentum % momenta_here

    mixed_ref[energies_all] = jnp.zeros(mixed_ref.shape[1:], jnp.float32)
    for energy in range(energies_all):
        blocks = [in_ref[place(energy, momentum)] for momentum in range(momenta_all)]
        for target in range(momenta_all):
            total = coefficient_ref[target, 0] * blocks[0]
            for momentum in range(1, momenta_all):
                total = total + coefficient_ref[target, momentum] * blocks[momentum]
            mixed_ref[energy, target] = total
    mask = mask_ref[...].astype(jnp.float32)
    for energy in range(energies_all):
        sources = []
        for branch in range(branches):
            below = energy - offset_ref[branch]
            above = energy + offset_ref[branch]
            below = jnp.where(jnp.logical_and(below >= 0, below < energies_all), below, energies_all)
            above = jnp.where(jnp.logical_and(above >= 0, above < energies_all), above, energies_all)
            sources.append((strength_ref[branch], below, above))
        for target in range(momenta_all):
            total = None
            for strength, below, above in sources:
                term = strength * (mixed_ref[below, target] + mixed_ref[above, target])
                total = term if total is None else total + term
            out_ref[place(energy, target)] = total * mask


def row_pieces(order_size, energy_groups, momentum_groups):
    per_energy = order_size // energy_groups
    piece_rows = parts * per_energy // momentum_groups
    pieces = []
    for energy_group in range(energy_groups):
        for momentum_group in range(momentum_groups):
            start, left, segments = momentum_group * piece_rows, piece_rows, []
            while left:
                part, inside = divmod(start, per_energy)
                count = min(left, per_energy - inside)
                segments.append((part, energy_group * per_energy + inside, count))
                start, left = start + count, left - count
            pieces.append(segments)
    return per_energy, piece_rows, pieces


def momentum_coefficients(momentum_table, momentum_weights):
    momentum_count = momentum_table.shape[0]
    labels = jnp.arange(momentum_count, dtype=jnp.int32)
    matches = momentum_table[:, :, None] == labels[None, None, :]
    return jnp.sum(jnp.where(matches, momentum_weights[None, :, None], 0.0), axis=1)


def product_split(left_side, right_side):
    return product(split_pair(left_side), split_pair(right_side))


def green_by_sweeps(hamiltonian, coupling, self_blocks, shift, position, slices):
    orbitals, surface = hamiltonian.shape[-1], coupling.shape[-1]
    corner = orbitals - surface
    identity = jnp.eye(orbitals, dtype=jnp.float32)
    symmetric = 0.5 * (hamiltonian + hamiltonian.T)
    system = jnp.stack(
        [
            shift[:, None, None] * identity - symmetric - self_blocks[:, 0],
            broadening * identity - self_blocks[:, 1],
        ],
        axis=1,
    )
    source = jnp.stack([jnp.zeros((surface, surface)), -contact * jnp.eye(surface)]).astype(jnp.float32)
    source = jnp.broadcast_to(source, (system.shape[0],) + source.shape)
    over_parts = jax.vmap(jax.vmap(product_split, (None, 0)), (None, 0))
    over_parts_right = jax.vmap(jax.vmap(product_split, (0, None)), (0, None))
    around = ((0, 0), (0, 0))

    def less_first(matrix, term):
        return matrix - jnp.pad(term, around + ((0, corner), (0, corner)))

    def less_last(matrix, term):
        return matrix - jnp.pad(term, around + ((corner, 0), (corner, 0)))

    def inverse(matrix):
        return jnp.stack(jax.vmap(inverse_pair)(matrix[:, 0], matrix[:, 1]), axis=1)

    def through(side, middle):
        return over_parts_right(over_parts(side, middle), side.T)

    left = source
    right = through(coupling, source)
    for turn in range(slices - 1):
        face = inverse(less_first(system, left))[..., corner:, corner:]
        moved = lax.ppermute(through(coupling.T, face), "space", [(i, i + 1) for i in range(slices - 1)])
        left = jnp.where(position == turn + 1, moved, left)
        face = inverse(less_last(system, right))[..., :surface, :surface]
        moved = lax.ppermute(face, "space", [(i + 1, i) for i in range(slices - 1)])
        right = jnp.where(position == slices - 2 - turn, through(coupling, moved), right)
    return inverse(less_last(less_first(system, left), right))


def cut_pieces(green, pieces):
    return jnp.stack(
        [
            jnp.concatenate([green[:, part, row : row + count] for part, row, count in segments], axis=1)
            for segments in pieces
        ]
    )


def on_chip(*block):
    return pl.BlockSpec(memory_space=pltpu.SMEM)


def resident(shape):
    return pl.BlockSpec(shape, lambda item: (0,) * len(shape))


def per_item(shape):
    return pl.BlockSpec((1,) + shape, lambda item: (item,) + (0,) * len(shape))


float_vmem = functools.partial(pltpu.VMEM, dtype=jnp.float32)
half_vmem = functools.partial(pltpu.VMEM, dtype=jnp.bfloat16)


def green_two_slices(hamiltonian, coupling, self_blocks, shift, position, pieces, blocks_shape):
    orbitals, surface = hamiltonian.shape[-1], coupling.shape[-1]
    items = self_blocks.shape[0]
    slice_now = position.astype(jnp.int32).reshape(1)
    order = (orbitals, orbitals)

    swap = [(0, 1), (1, 0)]
    first_coupling = lax.ppermute(coupling[0], "space", swap)
    first_coupling = jnp.where(position == 0, coupling[0], first_coupling)
    known, face = pl.pallas_call(
        functools.partial(start_kernel, surface),
        grid=(items,),
        in_specs=[
            on_chip(), on_chip(), resident((1,) + order), resident((1, surface, surface)), per_item((parts,) + order),
        ],
        out_specs=[per_item((parts,) + order), per_item((parts, surface, orbitals))],
        out_shape=[
            jax.ShapeDtypeStruct((items, parts) + order, jnp.float32),
            jax.ShapeDtypeStruct((items, parts, surface, orbitals), jnp.float32),
        ],
        scratch_shapes=[float_vmem(order), float_vmem(order), float_vmem(order), float_vmem((parts,) + order)],
        compiler_params=pltpu.CompilerParams(vmem_limit_bytes=kernel_memory),
        name="start",
    )(slice_now, shift, hamiltonian, coupling, self_blocks)
    face = lax.ppermute(face, "space", swap)

    return pl.pallas_call(
        functools.partial(finish_kernel, surface, pieces),
        grid=(items,),
        in_specs=[
            on_chip(), resident((surface, surface)), per_item((parts,) + order), per_item((parts, surface, orbitals)),
        ],
        out_specs=pl.BlockSpec((blocks_shape[0], 1) + blocks_shape[2:], lambda item: (0, item, 0, 0)),
        out_shape=jax.ShapeDtypeStruct(blocks_shape, jnp.float32),
        scratch_shapes=[float_vmem(order)] + [half_vmem(order)] * 4 + [float_vmem((parts,) + order)],
        compiler_params=pltpu.CompilerParams(vmem_limit_bytes=kernel_memory),
        name="finish",
    )(slice_now, first_coupling, known, face)


def body(
    hamiltonian,
    coupling,
    self_energy,
    pattern,
    momentum_table,
    momentum_weights,
    mode_strengths,
    mode_offsets,
):
    orbitals = hamiltonian.shape[-1]
    surface = coupling.shape[-1]
    energies_here = self_energy.shape[1]
    momenta_here = self_energy.shape[2]
    energy_groups = lax.axis_size("energy")
    momentum_groups = lax.axis_size("mom")
    position = lax.axis_index("space")
    energies_all = energies_here * energy_groups
    momenta_all = momenta_here * momentum_groups
    items = energies_here * momenta_here
    branches = mode_offsets.shape[0]
    energy_index = lax.axis_index("energy") * energies_here + jnp.arange(energies_here, dtype=jnp.int32)
    momentum_index = lax.axis_index("mom") * momenta_here + jnp.arange(momenta_here, dtype=jnp.int32)
    energy = -2.0 + 4.0 * energy_index.astype(jnp.float32) / energies_all
    angle = 2.0 * jnp.pi * momentum_index.astype(jnp.float32) / momenta_all
    kinetic = dispersion * (1.0 - jnp.cos(angle))
    shift = (energy[:, None] - kinetic[None, :]).reshape(items)
    self_blocks = self_energy.reshape(items, parts, orbitals, orbitals)
    per_energy, piece_rows, pieces = row_pieces(orbitals, energy_groups, momentum_groups)
    blocks_shape = (len(pieces), items, piece_rows, orbitals)
    if lax.axis_size("space") == 2:
        green = green_two_slices(hamiltonian, coupling, self_blocks, shift, position, pieces, blocks_shape)
    else:
        slices = lax.axis_size("space")
        green = green_by_sweeps(hamiltonian[0], coupling[0], self_blocks, shift, position, slices)
        green = cut_pieces(green, pieces)

    everyone = ("energy", "mom")
    gathered = lax.all_to_all(green, everyone, split_axis=0, concat_axis=0, tiled=True)
    coefficients = momentum_coefficients(momentum_table, momentum_weights)
    mask_rows = jnp.concatenate([pattern[0]] * parts, axis=0)
    mask_rows = lax.dynamic_slice_in_dim(mask_rows, lax.axis_index("mom") * piece_rows, piece_rows, 0)
    scattered = pl.pallas_call(
        functools.partial(
            scatter_kernel, energies_all, momenta_all, energies_here, momenta_here, momentum_groups, branches
        ),
        in_specs=[on_chip(), on_chip(), on_chip(), pl.BlockSpec(), pl.BlockSpec()],
        out_shape=jax.ShapeDtypeStruct(blocks_shape, jnp.float32),
        scratch_shapes=[float_vmem((energies_all + 1, momenta_all, piece_rows, orbitals))],
        compiler_params=pltpu.CompilerParams(vmem_limit_bytes=kernel_memory),
        name="scatter",
    )(mode_offsets, mode_strengths, coefficients, mask_rows, gathered)
    returned = lax.all_to_all(scattered, everyone, split_axis=0, concat_axis=0, tiled=True)
    returned = returned.reshape(energy_groups, momentum_groups, items, piece_rows, orbitals)
    returned = returned.transpose(2, 0, 1, 3, 4).reshape(items, energy_groups, parts, per_energy, orbitals)
    returned = returned.transpose(0, 2, 1, 3, 4)
    return returned.reshape(1, energies_here, momenta_here, parts, orbitals, orbitals)


def solution(mesh):
    return jax.shard_map(
        body,
        mesh=mesh,
        in_specs=(
            P("space", None, None),
            P("space", None, None),
            P("space", "energy", "mom", None, None, None),
            P("space", "energy", None),
            P(),
            P(),
            P(),
            P(),
        ),
        out_specs=P("space", "energy", "mom", None, None, None),
        check_vma=False,
    )
```

time: 276 us -> 80 us (0.29)
  local copies, waits for them, and re-layouts: 93.8 us -> 3.9 us
  waiting for transfers between devices: 76.4 us -> 26.2 us
  matrix products: 24 us -> 0 us
  between operations: 18.5 us -> 0.09 us
  other arithmetic: 13.6 us -> 1.12 us
  starting transfers between devices: 16.9 us -> 8.99 us
  Pallas kernels: 0 us -> 7.83 us
    squeeze x12 -> x0, local copies, waits for them, and re-layouts: 34.4 us -> none  [the longest x6 16.7 us: approximate_inverse(): real_part = matrix[..., 0, :, :]]
    ppermute x6 -> x2, waiting for transfers between devices: 34.6 us -> 2.35 us  [the longest x1 2.35 us: green_two_slices(): first_coupling = lax.ppermute(coupling[0], 'space', swap)]
    all_gather x1 -> x0, waiting for transfers between devices: 31.6 us -> none  [body(): lax.all_gather(phonon, 'mom', axis=1, tiled=True)]
    dot_general x30 -> x0, matrix products: 24 us -> none  [the longest x20 8.7 us: matmul_highest(): jnp.einsum('...ij,...jk->...ik', left_side, right_side, precision=lax.Pre...]
    scatter-add x6 -> x0, local copies, waits for them, and re-layouts: 23.7 us -> none  [the longest x3 13.8 us: embed_last(): return matrix.at[..., order_size - width:, order_size - width:].add(-term)]
    gather x12 -> x0, local copies, waits for them, and re-layouts: 23.6 us -> none  [the longest x6 11.8 us: approximate_inverse(): diag_imag = jnp.diagonal(imag_part, axis1=-2, axis2=-1)]
    all_to_all x1, waiting for transfers between devices: 10.2 us -> 23.8 us  [body(): lax.all_to_all(green, everyone, split_axis=0, concat_axis=0, tiled=True)]
    ppermute x6 -> x2, starting transfers between devices: 10 us -> 1 us  [the longest x1 0.93 us: green_two_slices(): face = lax.ppermute(face, 'space', swap)]
  transfers between devices with their start and end apart: 8 -> 3, of which waited for: 8 -> 2; matrix products, arithmetic and copies ran while one was open for 0% -> 1% of each run, Pallas kernels for 0% -> 0%
where the time goes in v1:
time: 80 us; the launch traced here: 79.6 us
  blocking collectives  31.5 us (39%)
  waiting for transfers between devices  26.2 us (33%)
  starting transfers between devices  8.99 us (11%)
  Pallas kernels  7.83 us (10%)
  local copies, waits for them, and re-layouts  3.9 us (5%)
  other arithmetic  1.12 us (1%)
    all_to_all x1, blocking collectives, body(): lax.all_to_all(scattered, everyone, split_axis=0, concat_axis=0, tiled=True)  31.5 us
    all_to_all x1, waiting for transfers between devices, body(): lax.all_to_all(green, everyone, split_axis=0, concat_axis=0, tiled=True)  23.8 us
    all_to_all x1, starting transfers between devices, body(): lax.all_to_all(green, everyone, split_axis=0, concat_axis=0, tiled=True)  7.99 us
    pallas_call x1, Pallas kernels, green_two_slices(): pl.pallas_call(functools.partial(finish_kernel, surface, pieces), grid=(i...  4.02 us
    unnamed x14, local copies, waits for them, and re-layouts  2.82 us
    pallas_call x1, Pallas kernels, green_two_slices(): pl.pallas_call(functools.partial(start_kernel, surface), grid=(items,), i...  2.74 us
    ppermute x1, waiting for transfers between devices, green_two_slices(): first_coupling = lax.ppermute(coupling[0], 'space', swap)  2.35 us
  transfers between devices with their start and end apart: 3, of which 2 were waited for; matrix products, arithmetic and copies ran while one was open for 1% of the time, Pallas kernels for 0%

profile of v1, /device:TPU:0, one launch (start us, length us, event | category | flops | bytes accessed | tf_op | source)
XLA Modules:
  0.0 79.6 jit_solution(13337591336564977565)
XLA Ops:
  0.0 0.0 copy-start
  0.1 1.2 %copy-done = f32[1,1,2,2,256,256]{5,4,3,2,1,0:T(8,128)S(1)} copy-done((f32[1,1,2,2,256,256]{5,4,3,2,1,0:T(8,128)S(1)}, f32[1,1,2,2,256,256]{5,4,3,2,1,0:T(8,128)}, u32[]{:S(2)}) %copy-start) | copy-done | bytes 1048600
  1.3 0.0 copy-start.1
  1.3 0.9 %copy-done.1 = f32[1,256,256]{2,1,0:T(8,128)S(1)} copy-done((f32[1,256,256]{2,1,0:T(8,128)S(1)}, f32[1,256,256]{2,1,0:T(8,128)}, u32[]{:S(2)}) %copy-start.1) | copy-done | bytes 262168
  2.2 2.7 %start.1 = (f32[2,2,256,256]{3,2,1,0:T(8,128)S(1)}, f32[2,2,224,256]{3,2,1,0:T(8,128)S(1)}) custom-call(s32[1]{0:T(128)} %bitcast.1.slice_ref, f32[2]{0:T(128)S(1)} %subtract_subtract_fusion.shift_ref, f32[1,256,256]{2,1,0:T(8,128)S(1)} %copy-done.1, f32[1,224,224]{2,1,0:T(8,128)} %coupling_ref.1, f32[2,2,256,256]{3,2,1,0:T(8,128)S(1)} %bitcast.9), custom_call_target="tpu_custom_call" | custom-call | tf_op jit(solution)/shard_map/start/pallas_call | solution.py:277
  5.0 0.9 %collective-permute-start.1 = (f32[2,2,224,256]{3,2,1,0:T(8,128)S(1)}, f32[2,2,224,256]{3,2,1,0:T(8,128)S(1)}, u32[]{:S(2)}, u32[]{:S(2)}) collective-permute-start(f32[2,2,224,256]{3,2,1,0:T(8,128)S(1)} %get-tuple-element.8), channel_id=1, source_target_pairs={{0,16},{16,0},{1,17},{17,1},{2,18},{18,2},{3,19},{19,3},{4,20},{20... | collective-permute-start | bytes 2752520 | tf_op jit(solution)/shard_map/ppermute | solution.py:292
  5.9 0.1 collective-permute-start
  6.0 2.3 %collective-permute-done = f32[224,224]{1,0:T(8,128)S(1)} collective-permute-done((f32[224,224]{1,0:T(8,128)}, f32[224,224]{1,0:T(8,128)S(1)}, u32[]{:S(2)}, u32[]{:S(2)}) %collective-permute-start) | collective-permute-done | bytes 200736 | tf_op jit(solution)/shard_map/ppermute | solution.py:275
  8.3 1.0 %broadcast_select_fusion.coupling_ref = f32[224,224]{1,0:T(8,128)S(1)} fusion(f32[224,224]{1,0:T(8,128)S(1)} %collective-permute-done, pred[]{:T(512)S(6)} %eq.19, f32[1,224,224]{2,1,0:T(8,128)} %coupling_ref.1), kind=kLoop, calls=%fused_computation | loop fusion | flops 50176 | bytes 602113 | tf_op jit(solution)/shard_map/jit(_where)/select_n | solution.py:276
  9.3 0.0 collective-permute-done.1.face_ref
  9.3 4.0 %finish.1 = f32[16,2,32,256]{3,2,1,0:T(8,128)} custom-call(s32[1]{0:T(128)} %bitcast.1.slice_ref, f32[224,224]{1,0:T(8,128)S(1)} %broadcast_select_fusion.coupling_ref, f32[2,2,256,256]{3,2,1,0:T(8,128)S(1)} %get-tuple-element.7.known_ref, f32[2,2,224,256]{3,2,1,0:T(8,128)S(1)} %collective-permute-done.1.face_ref), custom_call_target="tpu_custom_call" | custom-call | tf_op jit(solution)/shard_map/finish/pallas_call | solution.py:294
  13.3 0.0 copy-start.4
  13.3 8.0 %all-to-all-start = ((f32[16,2,32,256]{3,2,1,0:T(8,128)}), f32[16,2,32,256]{3,2,1,0:T(8,128)S(1)}, u32[]{:S(2)}, u32[]{:S(2)}) async-start(f32[16,2,32,256]{3,2,1,0:T(8,128)} %finish.1), calls=%async_computation | async-start | bytes 2097152 | tf_op jit(solution)/shard_map/all_to_all | solution.py:346
  21.3 0.0 copy-done.4
  21.3 0.0 copy-start.5
  21.4 0.0 copy-start.6
  21.4 0.6 copy-done.5
  22.0 0.0 copy-done.6
  22.0 0.0 copy-start.2
  22.0 0.0 copy-start.3
  22.0 0.1 select_reduce_fusion.coefficient_ref
  22.1 23.8 %all-to-all-done.in_ref = f32[16,2,32,256]{3,2,1,0:T(8,128)S(1)} async-done(((f32[16,2,32,256]{3,2,1,0:T(8,128)}), f32[16,2,32,256]{3,2,1,0:T(8,128)S(1)}, u32[]{:S(2)}, u32[]{:S(2)}) %all-to-all-start) | async-done | bytes 1048608 | tf_op jit(solution)/shard_map/all_to_all | solution.py:346
  45.9 0.0 copy-done.2
  46.0 0.0 copy-done.3
  46.0 1.1 %scatter.1 = f32[16,2,32,256]{3,2,1,0:T(8,128)S(1)} custom-call(s32[2]{0:T(128)S(1)} %copy-done.2, f32[2]{0:T(128)S(1)} %copy-done.3, f32[4,4]{1,0:T(4,128)S(1)} %select_reduce_fusion.coefficient_ref, s32[32,256]{1,0:T(8,128)S(1)} %fusion.mask_ref, f32[16,2,32,256]{3,2,1,0:T(8,128)S(1)} %all-to-all-done.in_ref), custom_call_target="tpu_custom_call" | custom-call | tf_op jit(solution)/shard_map/scatter/pallas_call | solution.py:350
  47.0 31.5 %all_to_all.10 = f32[16,2,32,256]{3,2,1,0:T(8,128)S(1)} all-to-all(f32[16,2,32,256]{3,2,1,0:T(8,128)S(1)} %scatter.1), channel_id=1, replica_groups=mesh['space'=2,'energy'=8,'mom'=2] {'energy','mom'}, dimensions={0} | all-to-all | bytes 2097152 | tf_op jit(solution)/shard_map/all_to_all | solution.py:360
  78.5 1.1 %copy.10 = f32[2,2,8,32,256]{4,3,2,1,0:T(8,128)} copy(f32[2,2,8,32,256]{4,3,0,1,2:T(8,128)S(1)} %bitcast.10) | data formatting | bytes 2097152 | tf_op jit(solution)/shard_map/transpose;transpose | solution.py:363
  (2 shorter events, 0.1 us)
Async XLA Ops:
  0.0 1.2 %copy-start = (f32[1,1,2,2,256,256]{5,4,3,2,1,0:T(8,128)S(1)}, f32[1,1,2,2,256,256]{5,4,3,2,1,0:T(8,128)}, u32[]{:S(2)}) copy-start(f32[1,1,2,2,256,256]{5,4,3,2,1,0:T(8,128)} %param.10) | copy-start | bytes 3145732
  1.3 0.9 %copy-start.1 = (f32[1,256,256]{2,1,0:T(8,128)S(1)}, f32[1,256,256]{2,1,0:T(8,128)}, u32[]{:S(2)}) copy-start(f32[1,256,256]{2,1,0:T(8,128)} %hamiltonian_ref.1) | copy-start | bytes 786436
  5.0 4.3 %collective-permute-start.1 = (f32[2,2,224,256]{3,2,1,0:T(8,128)S(1)}, f32[2,2,224,256]{3,2,1,0:T(8,128)S(1)}, u32[]{:S(2)}, u32[]{:S(2)}) collective-permute-start(f32[2,2,224,256]{3,2,1,0:T(8,128)S(1)} %get-tuple-element.8), channel_id=1, source_target_pairs={{0,16},{16,0},{1,17},{17,1},{2,18},{18,2},{3,19},{19,3},{4,20},{20... | collective-permute-start | bytes 2752520 | tf_op jit(solution)/shard_map/ppermute | solution.py:292
  5.9 2.4 %collective-permute-start = (f32[224,224]{1,0:T(8,128)}, f32[224,224]{1,0:T(8,128)S(1)}, u32[]{:S(2)}, u32[]{:S(2)}) collective-permute-start(f32[224,224]{1,0:T(8,128)} %bitcast.2), channel_id=1, source_target_pairs={{0,16},{16,0},{1,17},{17,1},{2,18},{18,2},{3,19},{19,3},{4,20},{20... | collective-permute-start | bytes 602120 | tf_op jit(solution)/shard_map/ppermute | solution.py:275
  13.3 8.0 %copy-start.4 = (s32[1,32,256]{2,1,0:T(8,128)S(1)}, s32[1,32,256]{2,1,0:T(8,128)}, u32[]{:S(2)}) copy-start(s32[1,32,256]{2,1,0:T(8,128)} %param.11) | copy-start | bytes 98308
  13.3 32.6 %all-to-all-start = ((f32[16,2,32,256]{3,2,1,0:T(8,128)}), f32[16,2,32,256]{3,2,1,0:T(8,128)S(1)}, u32[]{:S(2)}, u32[]{:S(2)}) async-start(f32[16,2,32,256]{3,2,1,0:T(8,128)} %finish.1), calls=%async_computation | async-start | bytes 2097152 | tf_op jit(solution)/shard_map/all_to_all | solution.py:346
  21.3 0.7 copy-start.5
  21.4 0.7 copy-start.6
  22.0 23.9 %copy-start.2 = (s32[2]{0:T(128)S(1)}, s32[2]{0:T(128)}, u32[]{:S(2)}) copy-start(s32[2]{0:T(128)} %offset_ref.1) | copy-start | bytes 28
  22.0 23.9 %copy-start.3 = (f32[2]{0:T(128)S(1)}, f32[2]{0:T(128)}, u32[]{:S(2)}) copy-start(f32[2]{0:T(128)} %strength_ref.1) | copy-start | bytes 28

commit v2 on v1

--- a/solution.py
+++ b/solution.py
@@ -32,20 +32,33 @@
     return rows == columns
 
 
+def product_stacked(left_pairs, right_pair):
+    rows = left_pairs[0][0].shape[0]
+    count = len(left_pairs)
+    right_high, right_low = right_pair
+    highs = [pair[0] for pair in left_pairs]
+    lows = [pair[1] for pair in left_pairs]
+    dot = functools.partial(jnp.dot, preferred_element_type=jnp.float32)
+    with_high = dot(jnp.concatenate(highs + lows, axis=0), right_high)
+    with_low = dot(jnp.concatenate(highs, axis=0), right_low)
+    return [
+        with_high[i * rows : (i + 1) * rows]
+        + with_high[(count + i) * rows : (count + i + 1) * rows]
+        + with_low[i * rows : (i + 1) * rows]
+        for i in range(count)
+    ]
+
+
 def inverse_pair(real_part, imag_part):
     order_size = real_part.shape[-1]
     on_diagonal = diagonal_mask(order_size)
-    only_real = jnp.where(on_diagonal, real_part, 0.0)
-    only_imag = jnp.where(on_diagonal, imag_part, 0.0)
-
-    def reciprocal(axis):
-        diag_real = jnp.sum(only_real, axis=axis, keepdims=True)
-        diag_imag = jnp.sum(only_imag, axis=axis, keepdims=True)
-        modulus = diag_real * diag_real + diag_imag * diag_imag
-        return diag_real / modulus, -diag_imag / modulus
-
-    row_real, row_imag = reciprocal(1)
-    column_real, column_imag = reciprocal(0)
+    diag_real = jnp.sum(jnp.where(on_diagonal, real_part, 0.0), axis=0, keepdims=True)
+    diag_imag = jnp.sum(jnp.where(on_diagonal, imag_part, 0.0), axis=0, keepdims=True)
+    modulus = diag_real * diag_real + diag_imag * diag_imag
+    column_real = diag_real / modulus
+    column_imag = -diag_imag / modulus
+    row_real = jnp.sum(jnp.where(on_diagonal, column_real, 0.0), axis=1, keepdims=True)
+    row_imag = jnp.sum(jnp.where(on_diagonal, column_imag, 0.0), axis=1, keepdims=True)
     off_real = jnp.where(on_diagonal, 0.0, real_part)
     off_imag = jnp.where(on_diagonal, 0.0, imag_part)
     scaled_real = row_real * off_real - row_imag * off_imag
@@ -53,9 +66,9 @@
     pair_real = split_pair(scaled_real)
     pair_imag = split_pair(scaled_imag)
     pair_both = split_pair(scaled_real + scaled_imag)
-    square_real = product(pair_real, pair_real)
-    square_imag = product(pair_imag, pair_imag)
-    square_both = product(pair_both, pair_both)
+    (square_real,) = product_stacked([pair_real], pair_real)
+    (square_imag,) = product_stacked([pair_imag], pair_imag)
+    (square_both,) = product_stacked([pair_both], pair_both)
     series_real = square_real - square_imag - scaled_real + jnp.where(on_diagonal, 1.0, 0.0)
     series_imag = square_both - square_real - square_imag - scaled_imag
     return (
@@ -64,78 +77,117 @@
     )
 
 
-def start_kernel(
-    surface, slice_ref, shift_ref, hamiltonian_ref, coupling_ref, self_ref, known_ref, face_ref,
-    base_ref, term_ref, wide_ref, green_ref,
-):
-    order_size = hamiltonian_ref.shape[-1]
+def start_kernel(item, items, surface, slice_ref, shift_ref, base_from_ref, term_from_ref, *rest):
+    slice_now = slice_ref[0]
+    if item == 0:
+        self_from_ref, known_ref, face_ref, base_ref, term_ref = rest[:5]
+        later_refs = rest[5 : 4 + items]
+        self_ref, green_ref, base_buffer, coupling_buffer, wide_ref, semaphores = rest[4 + items :]
+        self_copies = []
+        for place, target_ref in enumerate((self_ref,) + later_refs):
+            for part in range(parts):
+                semaphore = semaphores.at[2 + place * parts + part]
+                copy = pltpu.make_async_copy(self_from_ref.at[place, part], target_ref.at[part], semaphore)
+                self_copies.append(copy)
+        coupling_copy = pltpu.make_async_copy(term_from_ref.at[0], coupling_buffer, semaphores.at[0])
+        base_copy = pltpu.make_async_copy(base_from_ref.at[0], base_buffer, semaphores.at[1])
+        for copy in [coupling_copy, base_copy] + self_copies:
+            copy.start()
+    else:
+        self_ref, known_ref, face_ref, green_ref = rest
+        base_ref, term_ref = base_from_ref, term_from_ref
+    order_size = known_ref.shape[-1]
     corner = order_size - surface
-    item = pl.program_id(0)
-    slice_now = slice_ref[0]
-
-    @pl.when(item == 0)
-    def _():
-        base_ref[...] = 0.5 * (hamiltonian_ref[0] + hamiltonian_ref[0].T)
+    on_diagonal = diagonal_mask(order_size)
+    if item == 0:
+        coupling_copy.wait()
+        face_ref[parts] = jnp.zeros(face_ref.shape[1:], jnp.float32)
+        face_ref[parts, :, :surface] = coupling_buffer[...]
 
         @pl.when(slice_now == 0)
         def _():
             rows = lax.broadcasted_iota(jnp.int32, (order_size, order_size), 0)
-            inside = jnp.logical_and(diagonal_mask(order_size), rows < surface)
+            inside = jnp.logical_and(on_diagonal, rows < surface)
             term_ref[...] = jnp.where(inside, contact, 0.0)
 
         @pl.when(slice_now != 0)
         def _():
             wide_ref[...] = jnp.zeros_like(wide_ref)
-            wide_ref[corner:, :surface] = coupling_ref[0]
+            wide_ref[corner:, :surface] = coupling_buffer[...]
             wide = wide_ref[...]
             term_ref[...] = contact * product(split_pair(wide), split_pair(wide.T))
 
-    on_diagonal = diagonal_mask(order_size)
-    real_part = jnp.where(on_diagonal, shift_ref[item], 0.0) - base_ref[...] - self_ref[0, 0]
-    imag_part = jnp.where(on_diagonal, broadening, 0.0) - self_ref[0, 1] + term_ref[...]
-    known_ref[0, 0] = real_part
-    known_ref[0, 1] = imag_part
+        base_copy.wait()
+        base_ref[...] = 0.5 * (base_buffer[...] + base_buffer[...].T)
+        for copy in self_copies[:parts]:
+            copy.wait()
+    real_part = jnp.where(on_diagonal, shift_ref[item], 0.0) - base_ref[...] - self_ref[0]
+    imag_part = jnp.where(on_diagonal, broadening, 0.0) - self_ref[1] + term_ref[...]
+    known_ref[0] = real_part
+    known_ref[1] = imag_part
     green_real, green_imag = inverse_pair(real_part, imag_part)
     green_ref[0] = green_real
     green_ref[1] = green_imag
     first = pl.multiple_of(jnp.where(slice_now == 0, corner, 0), 8)
-    face_ref[0] = green_ref[:, pl.ds(first, surface), :]
-
-
-def finish_kernel(
-    surface, pieces, slice_ref, coupling_ref, known_ref, face_ref, out_ref,
-    wide_ref, side_high_ref, side_low_ref, across_high_ref, across_low_ref, face_full_ref,
-):
+    face_ref[:parts] = green_ref[:, pl.ds(first, surface), :]
+    if item == 0:
+        for copy in self_copies[parts:]:
+            copy.wait()
+
+
+def finish_kernel(item, items, surface, pieces, *refs):
+    last = item == items - 1
+    slice_ref, known_ref, face_ref = refs[:3]
+    refs = refs[3:]
+    if item == 0:
+        own_ref, refs = refs[0], refs[1:]
+    else:
+        sides, refs = refs[:4], refs[4:]
+    earlier_refs, refs = (refs[:item], refs[item:]) if last else ((), refs)
+    out_ref, refs = refs[0], refs[1:]
+    if item == 0:
+        sides, refs = refs[:4], refs[4:]
+    side_high_ref, side_low_ref, across_high_ref, across_low_ref = sides
+    face_full_ref = refs[0]
+    if item == 0:
+        wide_ref = refs[1]
     order_size = known_ref.shape[-1]
     corner = order_size - surface
-    item = pl.program_id(0)
     slice_now = slice_ref[0]
-
-    @pl.when(item == 0)
-    def _():
-        face_full_ref[...] = jnp.zeros_like(face_full_ref)
+    face_full_ref[...] = jnp.zeros_like(face_full_ref)
+    if item == 0:
         wide_ref[...] = jnp.zeros_like(wide_ref)
-        wide_ref[corner:, :surface] = coupling_ref[...]
-        plain = wide_ref[...]
-        turned = plain.T
-        at_first = slice_now == 0
-        side_high_ref[...], side_low_ref[...] = split_pair(jnp.where(at_first, plain, turned))
-        across_high_ref[...], across_low_ref[...] = split_pair(jnp.where(at_first, turned, plain))
+
+        @pl.when(slice_now == 0)
+        def _():
+            wide_ref[corner:, :surface] = own_ref[parts, :, :surface]
+            plain = wide_ref[...]
+            side_high_ref[...], side_low_ref[...] = split_pair(plain)
+            across_high_ref[...], across_low_ref[...] = split_pair(plain.T)
+
+        @pl.when(slice_now != 0)
+        def _():
+            wide_ref[corner:, :surface] = face_ref[parts, :, :surface]
+            plain = wide_ref[...]
+            side_high_ref[...], side_low_ref[...] = split_pair(plain.T)
+            across_high_ref[...], across_low_ref[...] = split_pair(plain)
 
     first = pl.multiple_of(jnp.where(slice_now == 0, 0, corner), 8)
-    face_full_ref[:, pl.ds(first, surface), :] = face_ref[0]
+    face_full_ref[:, pl.ds(first, surface), :] = face_ref[:parts]
     side = (side_high_ref[...], side_low_ref[...])
     across = (across_high_ref[...], across_low_ref[...])
-    through_real = product(side, split_pair(face_full_ref[0]))
-    through_imag = product(side, split_pair(face_full_ref[1]))
-    real_part = known_ref[0, 0] - product(split_pair(through_real), across)
-    imag_part = known_ref[0, 1] - product(split_pair(through_imag), across)
-    green = inverse_pair(real_part, imag_part)
+    (through_real,) = product_stacked([side], split_pair(face_full_ref[0]))
+    (through_imag,) = product_stacked([side], split_pair(face_full_ref[1]))
+    term_real, term_imag = product_stacked([split_pair(through_real), split_pair(through_imag)], across)
+    green = inverse_pair(known_ref[0] - term_real, known_ref[1] - term_imag)
     for piece, segments in enumerate(pieces):
         filled = 0
         for part, row, count in segments:
-            out_ref[piece, 0, filled : filled + count, :] = green[part][row : row + count, :]
+            target = (piece, item) if last else (piece,)
+            out_ref[target + (slice(filled, filled + count), slice(None))] = green[part][row : row + count, :]
             filled += count
+    for place, earlier_ref in enumerate(earlier_refs):
+        out_ref[:, place] = earlier_ref[...]
 
 
 def scatter_kernel(
@@ -253,16 +305,7 @@
     return pl.BlockSpec(memory_space=pltpu.SMEM)
 
 
-def resident(shape):
-    return pl.BlockSpec(shape, lambda item: (0,) * len(shape))
-
-
-def per_item(shape):
-    return pl.BlockSpec((1,) + shape, lambda item: (item,) + (0,) * len(shape))
-
-
 float_vmem = functools.partial(pltpu.VMEM, dtype=jnp.float32)
-half_vmem = functools.partial(pltpu.VMEM, dtype=jnp.bfloat16)
 
 
 def green_two_slices(hamiltonian, coupling, self_blocks, shift, position, pieces, blocks_shape):
@@ -270,39 +313,62 @@
     items = self_blocks.shape[0]
     slice_now = position.astype(jnp.int32).reshape(1)
     order = (orbitals, orbitals)
-
+    pair = (parts,) + order
+    floats = functools.partial(jax.ShapeDtypeStruct, dtype=jnp.float32)
+    halves = functools.partial(jax.ShapeDtypeStruct, dtype=jnp.bfloat16)
+    whole = pl.BlockSpec(memory_space=pltpu.VMEM)
+    far = pl.BlockSpec(memory_space=pltpu.HBM)
+    params = pltpu.CompilerParams(vmem_limit_bytes=kernel_memory)
+    inverse_flops = 18 * orbitals**3
     swap = [(0, 1), (1, 0)]
-    first_coupling = lax.ppermute(coupling[0], "space", swap)
-    first_coupling = jnp.where(position == 0, coupling[0], first_coupling)
-    known, face = pl.pallas_call(
-        functools.partial(start_kernel, surface),
-        grid=(items,),
-        in_specs=[
-            on_chip(), on_chip(), resident((1,) + order), resident((1, surface, surface)), per_item((parts,) + order),
-        ],
-        out_specs=[per_item((parts,) + order), per_item((parts, surface, orbitals))],
-        out_shape=[
-            jax.ShapeDtypeStruct((items, parts) + order, jnp.float32),
-            jax.ShapeDtypeStruct((items, parts, surface, orbitals), jnp.float32),
-        ],
-        scratch_shapes=[float_vmem(order), float_vmem(order), float_vmem(order), float_vmem((parts,) + order)],
-        compiler_params=pltpu.CompilerParams(vmem_limit_bytes=kernel_memory),
-        name="start",
-    )(slice_now, shift, hamiltonian, coupling, self_blocks)
-    face = lax.ppermute(face, "space", swap)
-
-    return pl.pallas_call(
-        functools.partial(finish_kernel, surface, pieces),
-        grid=(items,),
-        in_specs=[
-            on_chip(), resident((surface, surface)), per_item((parts,) + order), per_item((parts, surface, orbitals)),
-        ],
-        out_specs=pl.BlockSpec((blocks_shape[0], 1) + blocks_shape[2:], lambda item: (0, item, 0, 0)),
-        out_shape=jax.ShapeDtypeStruct(blocks_shape, jnp.float32),
-        scratch_shapes=[float_vmem(order)] + [half_vmem(order)] * 4 + [float_vmem((parts,) + order)],
-        compiler_params=pltpu.CompilerParams(vmem_limit_bytes=kernel_memory),
-        name="finish",
-    )(slice_now, first_coupling, known, face)
+
+    self_blocks, base, term = (
+        pltpu.with_memory_space_constraint(array, pltpu.HBM) for array in (self_blocks, hamiltonian, coupling)
+    )
+    known, faces, sent = [], [], []
+    later = []
+    for item in range(items):
+        first = item == 0
+        scratch = [float_vmem(pair)]
+        if first:
+            scratch += [float_vmem(pair), float_vmem(order), float_vmem((surface, surface)), float_vmem(order)]
+            scratch += [pltpu.SemaphoreType.DMA((2 + items * parts,))]
+        extra_shapes = [floats(order), floats(order)] + [floats(pair)] * (items - 1) if first else []
+        result = pl.pallas_call(
+            functools.partial(start_kernel, item, items, surface),
+            in_specs=[on_chip(), on_chip()] + [far if first else whole] * 3,
+            out_specs=[whole] * (2 + len(extra_shapes)),
+            out_shape=[floats(pair), floats((parts + first, surface, orbitals))] + extra_shapes,
+            scratch_shapes=scratch,
+            compiler_params=params,
+            cost_estimate=pl.CostEstimate(flops=inverse_flops, bytes_accessed=0, transcendentals=0),
+            name=f"start{item}",
+        )(slice_now, shift, base, term, self_blocks if first else later[item - 1])
+        known.append(result[0])
+        if first:
+            base, term, *later = result[2:]
+        sent.append(result[1])
+        faces.append(lax.ppermute(result[1], "space", swap))
+
+    greens, sides = [], []
+    for item in range(items):
+        first, last = item == 0, item == items - 1
+        operands = [slice_now, known[item], faces[item]] + ([sent[item]] if first else sides) + (greens if last else [])
+        out_shape = [floats(blocks_shape if last else blocks_shape[:1] + blocks_shape[2:])]
+        result = pl.pallas_call(
+            functools.partial(finish_kernel, item, items, surface, pieces),
+            in_specs=[on_chip()] + [whole] * (len(operands) - 1),
+            out_specs=[whole] * (5 if first else 1),
+            out_shape=out_shape + ([halves(order)] * 4 if first else []),
+            scratch_shapes=[float_vmem(pair)] + ([float_vmem(order)] if first else []),
+            compiler_params=params,
+            cost_estimate=pl.CostEstimate(flops=2 * inverse_flops, bytes_accessed=0, transcendentals=0),
+            name=f"finish{item}",
+        )(*operands)
+        greens.append(result[0])
+        if first:
+            sides = list(result[1:])
+    return greens[-1]
 
 
 def body(
@@ -343,10 +409,13 @@
         green = cut_pieces(green, pieces)
 
     everyone = ("energy", "mom")
-    gathered = lax.all_to_all(green, everyone, split_axis=0, concat_axis=0, tiled=True)
     coefficients = momentum_coefficients(momentum_table, momentum_weights)
     mask_rows = jnp.concatenate([pattern[0]] * parts, axis=0)
     mask_rows = lax.dynamic_slice_in_dim(mask_rows, lax.axis_index("mom") * piece_rows, piece_rows, 0)
+    green, coefficients, mask_rows, mode_offsets, mode_strengths = lax.optimization_barrier(
+        (green, coefficients, mask_rows, mode_offsets, mode_strengths)
+    )
+    gathered = lax.all_to_all(green, everyone, split_axis=0, concat_axis=0, tiled=True)
     scattered = pl.pallas_call(
         functools.partial(
             scatter_kernel, energies_all, momenta_all, energies_here, momenta_here, momentum_groups, branches

time: 80 us -> 75.5 us (0.944)
  blocking collectives: 31.5 us -> 63.8 us
  waiting for transfers between devices: 26.2 us -> 0.01 us
  starting transfers between devices: 8.99 us -> 0.88 us
  local copies, waits for them, and re-layouts: 3.9 us -> 1.74 us
  other arithmetic: 1.12 us -> 0.16 us
    all_to_all x0 -> x1, blocking collectives: none -> 34.4 us  [body(): lax.all_to_all(green, everyone, split_axis=0, concat_axis=0, tiled=True)]
    all_to_all x1 -> x0, waiting for transfers between devices: 23.8 us -> none  [body(): lax.all_to_all(green, everyone, split_axis=0, concat_axis=0, tiled=True)]
    all_to_all x1 -> x0, starting transfers between devices: 7.99 us -> none  [body(): lax.all_to_all(green, everyone, split_axis=0, concat_axis=0, tiled=True)]
    ppermute x2, waiting for transfers between devices: 2.35 us -> 0.01 us  [green_two_slices(): faces.append(lax.ppermute(result[1], 'space', swap))]
    unnamed x14 -> x10, local copies, waits for them, and re-layouts: 2.82 us -> 0.66 us
    all_to_all x1, blocking collectives: 31.5 us -> 29.4 us  [body(): lax.all_to_all(scattered, everyone, split_axis=0, concat_axis=0, tiled=True)]
    select_n x1 -> x0, other arithmetic: 0.97 us -> none  [green_two_slices(): first_coupling = jnp.where(position == 0, coupling[0], first_coupling)]
    pallas_call x2 -> x4, Pallas kernels: 6.76 us -> 7.51 us  [the longest x2 3.94 us: green_two_slices(): pl.pallas_call(functools.partial(start_kernel, item, items, surface), in_...]
  transfers between devices with their start and end apart: 3 -> 2, of which waited for: 2 -> 0; matrix products, arithmetic and copies ran while one was open for 1% -> 0% of each run, Pallas kernels for 0% -> 4%
where the time goes in v2:
time: 75.5 us; the launch traced here: 75.3 us
  blocking collectives  63.8 us (85%)
  Pallas kernels  8.58 us (11%)
  local copies, waits for them, and re-layouts  1.74 us (2%)
  starting transfers between devices  0.88 us (1%)
    all_to_all x1, blocking collectives, body(): lax.all_to_all(green, everyone, split_axis=0, concat_axis=0, tiled=True)  34.4 us
    all_to_all x1, blocking collectives, body(): lax.all_to_all(scattered, everyone, split_axis=0, concat_axis=0, tiled=True)  29.4 us
    pallas_call x2, Pallas kernels, green_two_slices(): pl.pallas_call(functools.partial(start_kernel, item, items, surface), in_...  3.94 us
    pallas_call x2, Pallas kernels, green_two_slices(): pl.pallas_call(functools.partial(finish_kernel, item, items, surface, pie...  3.57 us
  transfers between devices with their start and end apart: 2, of which 0 were waited for; matrix products, arithmetic and copies ran while one was open for 0% of the time, Pallas kernels for 4%

profile of v2, /device:TPU:0, one launch (start us, length us, event | category | flops | bytes accessed | tf_op | source)
XLA Modules:
  0.0 75.3 jit_solution(15043687802691601243)
XLA Ops:
  0.0 2.6 %start0.1 = (f32[2,256,256]{2,1,0:T(8,128)S(1)}, f32[3,224,256]{2,1,0:T(8,128)S(1)}, f32[256,256]{1,0:T(8,128)S(1)}, f32[256,256]{1,0:T(8,128)S(1)}, f32[2,256,256]{2,1,0:T(8,128)S(1)}) custom-call(s32[1]{0:T(128)} %bitcast.slice_ref.refs_0_, f32[2]{0:T(128)S(1)} %subtract_subtract_fusion.shift_ref, f32[1,256,256]{2,1,0:T(8,128)} %base_from_ref.1, ...), custom_call_target="tpu_custom_call" | custom-call | flops 301989888 | tf_op jit(solution)/shard_map/start0/pallas_call | solution.py:337
  2.7 0.8 %collective-permute-start.1 = (f32[3,224,256]{2,1,0:T(8,128)S(1)}, f32[3,224,256]{2,1,0:T(8,128)S(1)}, u32[]{:S(2)}, u32[]{:S(2)}) collective-permute-start(f32[3,224,256]{2,1,0:T(8,128)S(1)} %get-tuple-element.28.refs_3_), channel_id=1, source_target_pairs={{0,16},{16,0},{1,17},{17,1},{2,18},{18,2},{3,19},{19,3},{4,20},{20... | collective-permute-start | bytes 2064392 | tf_op jit(solution)/shard_map/ppermute | solution.py:351
  3.5 0.0 copy-start.2
  3.5 1.3 %start1.1 = (f32[2,256,256]{2,1,0:T(8,128)S(1)}, f32[2,224,256]{2,1,0:T(8,128)S(1)}) custom-call(s32[1]{0:T(128)} %bitcast.slice_ref.refs_0_, f32[2]{0:T(128)S(1)} %subtract_subtract_fusion.shift_ref, f32[256,256]{1,0:T(8,128)S(1)} %get-tuple-element.22.base_from_ref, f32[256,256]{1,0:T(8,128)S(1)} %get-tuple-element.23.term_from_ref, ...), custom_call_target="tpu_custom_call" | custom-call | flops 301989888 | tf_op jit(solution)/shard_map/start1/pallas_call | solution.py:337
  4.8 0.1 collective-permute-start
  4.9 0.0 copy-done.2
  4.9 0.0 copy-start.3
  4.9 0.0 copy-start.4
  4.9 0.6 copy-done.3
  5.6 0.0 copy-done.4
  5.6 0.1 select_reduce_fusion.coefficient_ref
  5.7 0.0 collective-permute-done.1.refs_2_
  5.7 1.8 %finish0.1 = (f32[16,32,256]{2,1,0:T(8,128)S(1)}, bf16[256,256]{1,0:T(8,128)(2,1)S(1)}, bf16[256,256]{1,0:T(8,128)(2,1)S(1)}, bf16[256,256]{1,0:T(8,128)(2,1)S(1)}, bf16[256,256]{1,0:T(8,128)(2,1)S(1)}) custom-call(s32[1]{0:T(128)} %bitcast.slice_ref.refs_0_, f32[2,256,256]{2,1,0:T(8,128)S(1)} %get-tuple-element.27.refs_1_, ...), custom_call_target="tpu_custom_call" | custom-call | flops 603979776 | tf_op jit(solution)/shard_map/finish0/pallas_call | solution.py:358
  7.5 0.0 collective-permute-done.refs_2_
  7.5 1.7 %finish1.1 = f32[16,2,32,256]{3,2,1,0:T(8,128)S(1)} custom-call(s32[1]{0:T(128)} %bitcast.slice_ref.refs_0_, f32[2,256,256]{2,1,0:T(8,128)S(1)} %get-tuple-element.25.refs_1_, f32[2,224,256]{2,1,0:T(8,128)S(1)} %collective-permute-done.refs_2_, bf16[256,256]{1,0:T(8,128)(2,1)S(1)} %get-tuple-element.29.refs_3_, ...), custom_call_target="tpu_custom_call" | custom-call | flops 603979776 | tf_op jit(solution)/shard_map/finish1/pallas_call | solution.py:358
  9.3 0.0 copy-start
  9.3 0.0 copy-start.1
  9.3 34.4 %all_to_all.10.in_ref = f32[16,2,32,256]{3,2,1,0:T(8,128)S(1)} all-to-all(f32[16,2,32,256]{3,2,1,0:T(8,128)S(1)} %finish1.1), channel_id=1, replica_groups=mesh['space'=2,'energy'=8,'mom'=2] {'energy','mom'}, dimensions={0} | all-to-all | bytes 2097152 | tf_op jit(solution)/shard_map/all_to_all | solution.py:418
  43.7 0.0 copy-done
  43.7 0.0 copy-done.1
  43.7 1.1 %scatter.1 = f32[16,2,32,256]{3,2,1,0:T(8,128)S(1)} custom-call(s32[2]{0:T(128)S(1)} %copy-done, f32[2]{0:T(128)S(1)} %copy-done.1, f32[4,4]{1,0:T(4,128)S(1)} %select_reduce_fusion.coefficient_ref, s32[32,256]{1,0:T(8,128)S(1)} %fusion.mask_ref, f32[16,2,32,256]{3,2,1,0:T(8,128)S(1)} %all_to_all.10.in_ref), custom_call_target="tpu_custom_call" | custom-call | tf_op jit(solution)/shard_map/scatter/pallas_call | solution.py:419
  44.8 29.4 %all_to_all.11 = f32[16,2,32,256]{3,2,1,0:T(8,128)S(1)} all-to-all(f32[16,2,32,256]{3,2,1,0:T(8,128)S(1)} %scatter.1), channel_id=1, replica_groups=mesh['space'=2,'energy'=8,'mom'=2] {'energy','mom'}, dimensions={0} | all-to-all | bytes 2097152 | tf_op jit(solution)/shard_map/all_to_all | solution.py:429
  74.2 1.1 %copy.10 = f32[2,2,8,32,256]{4,3,2,1,0:T(8,128)} copy(f32[2,2,8,32,256]{4,3,0,1,2:T(8,128)S(1)} %bitcast.7) | data formatting | bytes 2097152 | tf_op jit(solution)/shard_map/transpose;transpose | solution.py:432
  (2 shorter events, 0.1 us)
Async XLA Ops:
  2.7 3.0 %collective-permute-start.1 = (f32[3,224,256]{2,1,0:T(8,128)S(1)}, f32[3,224,256]{2,1,0:T(8,128)S(1)}, u32[]{:S(2)}, u32[]{:S(2)}) collective-permute-start(f32[3,224,256]{2,1,0:T(8,128)S(1)} %get-tuple-element.28.refs_3_), channel_id=1, source_target_pairs={{0,16},{16,0},{1,17},{17,1},{2,18},{18,2},{3,19},{19,3},{4,20},{20... | collective-permute-start | bytes 2064392 | tf_op jit(solution)/shard_map/ppermute | solution.py:351
  3.5 1.4 %copy-start.2 = (s32[1,32,256]{2,1,0:T(8,128)S(1)}, s32[1,32,256]{2,1,0:T(8,128)}, u32[]{:S(2)}) copy-start(s32[1,32,256]{2,1,0:T(8,128)} %param.11) | copy-start | bytes 98308
  4.8 2.7 %collective-permute-start = (f32[2,224,256]{2,1,0:T(8,128)S(1)}, f32[2,224,256]{2,1,0:T(8,128)S(1)}, u32[]{:S(2)}, u32[]{:S(2)}) collective-permute-start(f32[2,224,256]{2,1,0:T(8,128)S(1)} %get-tuple-element.26), channel_id=1, source_target_pairs={{0,16},{16,0},{1,17},{17,1},{2,18},{18,2},{3,19},{19,3},{4,20},{20... | collective-permute-start | bytes 1376264 | tf_op jit(solution)/shard_map/ppermute | solution.py:351
  4.9 0.7 copy-start.3
  4.9 0.7 copy-start.4
  9.3 34.5 %copy-start = (s32[2]{0:T(128)S(1)}, s32[2]{0:T(128)}, u32[]{:S(2)}) copy-start(s32[2]{0:T(128)} %offset_ref) | copy-start | bytes 28
  9.3 34.5 %copy-start.1 = (f32[2]{0:T(128)S(1)}, f32[2]{0:T(128)}, u32[]{:S(2)}) copy-start(f32[2]{0:T(128)} %strength_ref) | copy-start | bytes 28

commit v3 on v2

--- a/solution.py
+++ b/solution.py
@@ -2,6 +2,7 @@
 
 import jax
 import jax.numpy as jnp
+import numpy as np
 from jax import lax
 from jax.experimental import pallas as pl
 from jax.experimental.pallas import tpu as pltpu
@@ -12,6 +13,7 @@
 dispersion = 1.0
 parts = 2
 kernel_memory = 24 * 1024 * 1024
+member_seed = 29
 
 
 def split_pair(value):
@@ -191,12 +193,12 @@
 
 
 def scatter_kernel(
-    energies_all, momenta_all, energies_here, momenta_here, momentum_groups, branches,
+    energies_all, momenta_all, energies_here, momenta_here, momentum_groups, branches, slots,
     offset_ref, strength_ref, coefficient_ref, mask_ref, in_ref, out_ref, mixed_ref,
 ):
     def place(energy, momentum):
         group = (energy // energies_here) * momentum_groups + momentum // momenta_here
-        return group, (energy % energies_here) * momenta_here + momentum % momenta_here
+        return slots[group], (energy % energies_here) * momenta_here + momentum % momenta_here
 
     mixed_ref[energies_all] = jnp.zeros(mixed_ref.shape[1:], jnp.float32)
     for energy in range(energies_all):
@@ -223,6 +225,26 @@
             out_ref[place(energy, target)] = total * mask
 
 
+def assemble_kernel(pieces, in_ref, out_ref, semaphores):
+    copies = []
+    for item in range(out_ref.shape[0]):
+        for slot, segments in enumerate(pieces):
+            filled = 0
+            for part, row, count in segments:
+                source = in_ref.at[slot, item, pl.ds(filled, count)]
+                target = out_ref.at[item, part, pl.ds(row, count)]
+                copies.append(pltpu.make_async_copy(source, target, semaphores.at[len(copies)]))
+                filled += count
+    for copy in copies:
+        copy.start()
+    for copy in copies:
+        copy.wait()
+
+
+def member_order(count):
+    return [int(member) for member in np.random.RandomState(member_seed).permutation(count)]
+
+
 def row_pieces(order_size, energy_groups, momentum_groups):
     per_energy = order_size // energy_groups
     piece_rows = parts * per_energy // momentum_groups
@@ -236,7 +258,7 @@
                 segments.append((part, energy_group * per_energy + inside, count))
                 start, left = start + count, left - count
             pieces.append(segments)
-    return per_energy, piece_rows, pieces
+    return piece_rows, pieces
 
 
 def momentum_coefficients(momentum_table, momentum_weights):
@@ -399,7 +421,10 @@
     kinetic = dispersion * (1.0 - jnp.cos(angle))
     shift = (energy[:, None] - kinetic[None, :]).reshape(items)
     self_blocks = self_energy.reshape(items, parts, orbitals, orbitals)
-    per_energy, piece_rows, pieces = row_pieces(orbitals, energy_groups, momentum_groups)
+    piece_rows, pieces = row_pieces(orbitals, energy_groups, momentum_groups)
+    members = member_order(len(pieces))
+    slots = [members.index(group) for group in range(len(members))]
+    pieces = [pieces[member] for member in members]
     blocks_shape = (len(pieces), items, piece_rows, orbitals)
     if lax.axis_size("space") == 2:
         green = green_two_slices(hamiltonian, coupling, self_blocks, shift, position, pieces, blocks_shape)
@@ -408,17 +433,24 @@
         green = green_by_sweeps(hamiltonian[0], coupling[0], self_blocks, shift, position, slices)
         green = cut_pieces(green, pieces)
 
-    everyone = ("energy", "mom")
+    exchange = functools.partial(
+        lax.all_to_all,
+        axis_name=("energy", "mom"),
+        split_axis=0,
+        concat_axis=0,
+        axis_index_groups=[members],
+        tiled=True,
+    )
     coefficients = momentum_coefficients(momentum_table, momentum_weights)
     mask_rows = jnp.concatenate([pattern[0]] * parts, axis=0)
     mask_rows = lax.dynamic_slice_in_dim(mask_rows, lax.axis_index("mom") * piece_rows, piece_rows, 0)
     green, coefficients, mask_rows, mode_offsets, mode_strengths = lax.optimization_barrier(
         (green, coefficients, mask_rows, mode_offsets, mode_strengths)
     )
-    gathered = lax.all_to_all(green, everyone, split_axis=0, concat_axis=0, tiled=True)
+    gathered = exchange(green)
     scattered = pl.pallas_call(
         functools.partial(
-            scatter_kernel, energies_all, momenta_all, energies_here, momenta_here, momentum_groups, branches
+            scatter_kernel, energies_all, momenta_all, energies_here, momenta_here, momentum_groups, branches, slots
         ),
         in_specs=[on_chip(), on_chip(), on_chip(), pl.BlockSpec(), pl.BlockSpec()],
         out_shape=jax.ShapeDtypeStruct(blocks_shape, jnp.float32),
@@ -426,11 +458,18 @@
         compiler_params=pltpu.CompilerParams(vmem_limit_bytes=kernel_memory),
         name="scatter",
     )(mode_offsets, mode_strengths, coefficients, mask_rows, gathered)
-    returned = lax.all_to_all(scattered, everyone, split_axis=0, concat_axis=0, tiled=True)
-    returned = returned.reshape(energy_groups, momentum_groups, items, piece_rows, orbitals)
-    returned = returned.transpose(2, 0, 1, 3, 4).reshape(items, energy_groups, parts, per_energy, orbitals)
-    returned = returned.transpose(0, 2, 1, 3, 4)
-    return returned.reshape(1, energies_here, momenta_here, parts, orbitals, orbitals)
+    returned = exchange(scattered)
+    copies = items * sum(len(segments) for segments in pieces)
+    whole = pl.pallas_call(
+        functools.partial(assemble_kernel, pieces),
+        in_specs=[pl.BlockSpec(memory_space=pltpu.VMEM)],
+        out_specs=pl.BlockSpec(memory_space=pltpu.HBM),
+        out_shape=jax.ShapeDtypeStruct((items, parts, orbitals, orbitals), jnp.float32),
+        scratch_shapes=[pltpu.SemaphoreType.DMA((copies,))],
+        compiler_params=pltpu.CompilerParams(vmem_limit_bytes=kernel_memory),
+        name="assemble",
+    )(returned)
+    return whole.reshape(1, energies_here, momenta_here, parts, orbitals, orbitals)
 
 
 def solution(mesh):

time: 75.5 us -> 72.7 us (0.963)
  blocking collectives: 63.8 us -> 60.8 us
  Pallas kernels: 8.58 us -> 9.8 us
  local copies, waits for them, and re-layouts: 1.74 us -> 0.66 us
    all_to_all x2, blocking collectives: 63.8 us -> 60.8 us  [the longest x1 32.9 us: body(): gathered = exchange(green)]
    pallas_call x0 -> x1, Pallas kernels: none -> 1.23 us  [body(): pl.pallas_call(functools.partial(assemble_kernel, pieces), in_specs=[pl.B...]
    another operation x1 -> x0, local copies, waits for them, and re-layouts: 1.08 us -> none  [body(): returned = returned.transpose(0, 2, 1, 3, 4)]
where the time goes in v3:
time: 72.7 us; the launch traced here: 72.4 us
  blocking collectives  60.8 us (84%)
  Pallas kernels  9.8 us (13%)
  starting transfers between devices  0.88 us (1%)
    all_to_all x1, blocking collectives, body(): gathered = exchange(green)  32.9 us
    all_to_all x1, blocking collectives, body(): returned = exchange(scattered)  28 us
    pallas_call x2, Pallas kernels, green_two_slices(): pl.pallas_call(functools.partial(start_kernel, item, items, surface), in_...  3.94 us
    pallas_call x2, Pallas kernels, green_two_slices(): pl.pallas_call(functools.partial(finish_kernel, item, items, surface, pie...  3.57 us
  transfers between devices with their start and end apart: 2, of which 0 were waited for; matrix products, arithmetic and copies ran while one was open for 0% of the time, Pallas kernels for 4%

profile of v3, /device:TPU:0, one launch (start us, length us, event | category | flops | bytes accessed | tf_op | source)
XLA Modules:
  0.0 72.4 jit_solution(15854388651919141850)
XLA Ops:
  0.0 2.6 %start0.1 = (f32[2,256,256]{2,1,0:T(8,128)S(1)}, f32[3,224,256]{2,1,0:T(8,128)S(1)}, f32[256,256]{1,0:T(8,128)S(1)}, f32[256,256]{1,0:T(8,128)S(1)}, f32[2,256,256]{2,1,0:T(8,128)S(1)}) custom-call(s32[1]{0:T(128)} %bitcast.slice_ref.refs_0_, f32[2]{0:T(128)S(1)} %subtract_subtract_fusion.shift_ref, f32[1,256,256]{2,1,0:T(8,128)} %base_from_ref.1, ...), custom_call_target="tpu_custom_call" | custom-call | flops 301989888 | tf_op jit(solution)/shard_map/start0/pallas_call | solution.py:359
  2.7 0.8 %collective-permute-start.1 = (f32[3,224,256]{2,1,0:T(8,128)S(1)}, f32[3,224,256]{2,1,0:T(8,128)S(1)}, u32[]{:S(2)}, u32[]{:S(2)}) collective-permute-start(f32[3,224,256]{2,1,0:T(8,128)S(1)} %get-tuple-element.28.refs_3_), channel_id=1, source_target_pairs={{0,16},{16,0},{1,17},{17,1},{2,18},{18,2},{3,19},{19,3},{4,20},{20... | collective-permute-start | bytes 2064392 | tf_op jit(solution)/shard_map/ppermute | solution.py:373
  3.5 0.0 copy-start.2
  3.5 1.3 %start1.1 = (f32[2,256,256]{2,1,0:T(8,128)S(1)}, f32[2,224,256]{2,1,0:T(8,128)S(1)}) custom-call(s32[1]{0:T(128)} %bitcast.slice_ref.refs_0_, f32[2]{0:T(128)S(1)} %subtract_subtract_fusion.shift_ref, f32[256,256]{1,0:T(8,128)S(1)} %get-tuple-element.22.base_from_ref, f32[256,256]{1,0:T(8,128)S(1)} %get-tuple-element.23.term_from_ref, ...), custom_call_target="tpu_custom_call" | custom-call | flops 301989888 | tf_op jit(solution)/shard_map/start1/pallas_call | solution.py:359
  4.8 0.1 collective-permute-start
  4.9 0.0 copy-done.2
  4.9 0.0 copy-start.3
  4.9 0.0 copy-start.4
  4.9 0.6 copy-done.3
  5.6 0.0 copy-done.4
  5.6 0.1 select_reduce_fusion.coefficient_ref
  5.7 0.0 collective-permute-done.1.refs_2_
  5.7 1.8 %finish0.1 = (f32[16,32,256]{2,1,0:T(8,128)S(1)}, bf16[256,256]{1,0:T(8,128)(2,1)S(1)}, bf16[256,256]{1,0:T(8,128)(2,1)S(1)}, bf16[256,256]{1,0:T(8,128)(2,1)S(1)}, bf16[256,256]{1,0:T(8,128)(2,1)S(1)}) custom-call(s32[1]{0:T(128)} %bitcast.slice_ref.refs_0_, f32[2,256,256]{2,1,0:T(8,128)S(1)} %get-tuple-element.27.refs_1_, ...), custom_call_target="tpu_custom_call" | custom-call | flops 603979776 | tf_op jit(solution)/shard_map/finish0/pallas_call | solution.py:380
  7.5 0.0 collective-permute-done.refs_2_
  7.5 1.7 %finish1.1 = f32[16,2,32,256]{3,2,1,0:T(8,128)S(1)} custom-call(s32[1]{0:T(128)} %bitcast.slice_ref.refs_0_, f32[2,256,256]{2,1,0:T(8,128)S(1)} %get-tuple-element.25.refs_1_, f32[2,224,256]{2,1,0:T(8,128)S(1)} %collective-permute-done.refs_2_, bf16[256,256]{1,0:T(8,128)(2,1)S(1)} %get-tuple-element.29.refs_3_, ...), custom_call_target="tpu_custom_call" | custom-call | flops 603979776 | tf_op jit(solution)/shard_map/finish1/pallas_call | solution.py:380
  9.3 0.0 copy-start
  9.3 0.0 copy-start.1
  9.3 32.9 %all_to_all.10.in_ref = f32[16,2,32,256]{3,2,1,0:T(8,128)S(1)} all-to-all(f32[16,2,32,256]{3,2,1,0:T(8,128)S(1)} %finish1.1), channel_id=1, replica_groups={{4,7,6,13,11,14,15,10,1,9,0,8,2,12,3,5},{20,23,22,29,27,30,31,26,17,25,..., dimensions={0} | all-to-all | bytes 2097152 | tf_op jit(solution)/shard_map/all_to_all | solution.py:450
  42.1 0.0 copy-done
  42.1 0.0 copy-done.1
  42.2 1.1 %scatter.1 = f32[16,2,32,256]{3,2,1,0:T(8,128)S(1)} custom-call(s32[2]{0:T(128)S(1)} %copy-done, f32[2]{0:T(128)S(1)} %copy-done.1, f32[4,4]{1,0:T(4,128)S(1)} %select_reduce_fusion.coefficient_ref, s32[32,256]{1,0:T(8,128)S(1)} %fusion.mask_ref, f32[16,2,32,256]{3,2,1,0:T(8,128)S(1)} %all_to_all.10.in_ref), custom_call_target="tpu_custom_call" | custom-call | tf_op jit(solution)/shard_map/scatter/pallas_call | solution.py:451
  43.2 28.0 %all_to_all.11.in_ref = f32[16,2,32,256]{3,2,1,0:T(8,128)S(1)} all-to-all(f32[16,2,32,256]{3,2,1,0:T(8,128)S(1)} %scatter.1), channel_id=1, replica_groups={{4,7,6,13,11,14,15,10,1,9,0,8,2,12,3,5},{20,23,22,29,27,30,31,26,17,25,..., dimensions={0} | all-to-all | bytes 2097152 | tf_op jit(solution)/shard_map/all_to_all | solution.py:461
  71.2 1.2 %assemble.1 = f32[2,2,256,256]{3,2,1,0:T(8,128)} custom-call(f32[16,2,32,256]{3,2,1,0:T(8,128)S(1)} %all_to_all.11.in_ref), custom_call_target="tpu_custom_call" | custom-call | tf_op jit(solution)/shard_map/assemble/pallas_call | solution.py:463
  (2 shorter events, 0.1 us)
Async XLA Ops:
  2.7 3.0 %collective-permute-start.1 = (f32[3,224,256]{2,1,0:T(8,128)S(1)}, f32[3,224,256]{2,1,0:T(8,128)S(1)}, u32[]{:S(2)}, u32[]{:S(2)}) collective-permute-start(f32[3,224,256]{2,1,0:T(8,128)S(1)} %get-tuple-element.28.refs_3_), channel_id=1, source_target_pairs={{0,16},{16,0},{1,17},{17,1},{2,18},{18,2},{3,19},{19,3},{4,20},{20... | collective-permute-start | bytes 2064392 | tf_op jit(solution)/shard_map/ppermute | solution.py:373
  3.5 1.4 %copy-start.2 = (s32[1,32,256]{2,1,0:T(8,128)S(1)}, s32[1,32,256]{2,1,0:T(8,128)}, u32[]{:S(2)}) copy-start(s32[1,32,256]{2,1,0:T(8,128)} %param.11) | copy-start | bytes 98308
  4.8 2.7 %collective-permute-start = (f32[2,224,256]{2,1,0:T(8,128)S(1)}, f32[2,224,256]{2,1,0:T(8,128)S(1)}, u32[]{:S(2)}, u32[]{:S(2)}) collective-permute-start(f32[2,224,256]{2,1,0:T(8,128)S(1)} %get-tuple-element.26), channel_id=1, source_target_pairs={{0,16},{16,0},{1,17},{17,1},{2,18},{18,2},{3,19},{19,3},{4,20},{20... | collective-permute-start | bytes 1376264 | tf_op jit(solution)/shard_map/ppermute | solution.py:373
  4.9 0.7 copy-start.3
  4.9 0.7 copy-start.4
  9.3 32.9 %copy-start = (s32[2]{0:T(128)S(1)}, s32[2]{0:T(128)}, u32[]{:S(2)}) copy-start(s32[2]{0:T(128)} %offset_ref) | copy-start | bytes 28
  9.3 32.9 %copy-start.1 = (f32[2]{0:T(128)S(1)}, f32[2]{0:T(128)}, u32[]{:S(2)}) copy-start(f32[2]{0:T(128)} %strength_ref) | copy-start | bytes 28

commit v4 on v3

--- a/solution.py
+++ b/solution.py
@@ -13,7 +13,7 @@
 dispersion = 1.0
 parts = 2
 kernel_memory = 24 * 1024 * 1024
-member_seed = 29
+member_seed = 117
 
 
 def split_pair(value):
@@ -79,12 +79,33 @@
     )
 
 
+def write_factors(factor_ref, table_ref, weight_ref, strength_ref, offset_ref):
+    momenta_all, branches = weight_ref.shape[0], strength_ref.shape[0]
+    values = []
+    for target in range(momenta_all):
+        for source in range(momenta_all):
+            total = jnp.float32(0.0)
+            for transfer in range(momenta_all):
+                total += jnp.where(table_ref[target, transfer] == source, weight_ref[transfer], 0.0)
+            values.append(total)
+    values += [strength_ref[branch] for branch in range(branches)]
+    values += [offset_ref[branch].astype(jnp.float32) for branch in range(branches)]
+    for place, value in enumerate(values):
+        factor_ref[place] = jnp.full(factor_ref.shape[1:], value, jnp.float32)
+
+
 def start_kernel(item, items, surface, slice_ref, shift_ref, base_from_ref, term_from_ref, *rest):
     slice_now = slice_ref[0]
     if item == 0:
-        self_from_ref, known_ref, face_ref, base_ref, term_ref = rest[:5]
-        later_refs = rest[5 : 4 + items]
-        self_ref, green_ref, base_buffer, coupling_buffer, wide_ref, semaphores = rest[4 + items :]
+        self_from_ref, small_refs = rest[0], rest[1:5]
+        known_ref, face_ref, base_ref, term_ref, factor_ref = rest[5:10]
+        later_refs = rest[10 : 9 + items]
+        self_ref, base_buffer, coupling_buffer, wide_ref = rest[9 + items : 13 + items]
+        near_refs, semaphores, small_semaphores = rest[13 + items : 17 + items], rest[-2], rest[-1]
+        small_copies = [
+            pltpu.make_async_copy(small_ref, near_ref, small_semaphores.at[place])
+            for place, (small_ref, near_ref) in enumerate(zip(small_refs, near_refs))
+        ]
         self_copies = []
         for place, target_ref in enumerate((self_ref,) + later_refs):
             for part in range(parts):
@@ -93,10 +114,10 @@
                 self_copies.append(copy)
         coupling_copy = pltpu.make_async_copy(term_from_ref.at[0], coupling_buffer, semaphores.at[0])
         base_copy = pltpu.make_async_copy(base_from_ref.at[0], base_buffer, semaphores.at[1])
-        for copy in [coupling_copy, base_copy] + self_copies:
+        for copy in [coupling_copy, base_copy] + self_copies[:parts] + small_copies + self_copies[parts:]:
             copy.start()
     else:
-        self_ref, known_ref, face_ref, green_ref = rest
+        self_ref, known_ref, face_ref = rest
         base_ref, term_ref = base_from_ref, term_from_ref
     order_size = known_ref.shape[-1]
     corner = order_size - surface
@@ -128,13 +149,21 @@
     known_ref[0] = real_part
     known_ref[1] = imag_part
     green_real, green_imag = inverse_pair(real_part, imag_part)
-    green_ref[0] = green_real
-    green_ref[1] = green_imag
-    first = pl.multiple_of(jnp.where(slice_now == 0, corner, 0), 8)
-    face_ref[:parts] = green_ref[:, pl.ds(first, surface), :]
-    if item == 0:
-        for copy in self_copies[parts:]:
+
+    @pl.when(slice_now == 0)
+    def _():
+        face_ref[0] = green_real[corner:]
+        face_ref[1] = green_imag[corner:]
+
+    @pl.when(slice_now != 0)
+    def _():
+        face_ref[0] = green_real[:surface]
+        face_ref[1] = green_imag[:surface]
+
+    if item == 0:
+        for copy in small_copies + self_copies[parts:]:
             copy.wait()
+        write_factors(factor_ref, *near_refs)
 
 
 def finish_kernel(item, items, surface, pieces, *refs):
@@ -150,13 +179,11 @@
     if item == 0:
         sides, refs = refs[:4], refs[4:]
     side_high_ref, side_low_ref, across_high_ref, across_low_ref = sides
-    face_full_ref = refs[0]
-    if item == 0:
-        wide_ref = refs[1]
+    if item == 0:
+        wide_ref = refs[0]
     order_size = known_ref.shape[-1]
     corner = order_size - surface
     slice_now = slice_ref[0]
-    face_full_ref[...] = jnp.zeros_like(face_full_ref)
     if item == 0:
         wide_ref[...] = jnp.zeros_like(wide_ref)
 
@@ -164,22 +191,22 @@
         def _():
             wide_ref[corner:, :surface] = own_ref[parts, :, :surface]
             plain = wide_ref[...]
-            side_high_ref[...], side_low_ref[...] = split_pair(plain)
+            side_high_ref[...], side_low_ref[...] = split_pair(plain[:, :surface])
             across_high_ref[...], across_low_ref[...] = split_pair(plain.T)
 
         @pl.when(slice_now != 0)
         def _():
             wide_ref[corner:, :surface] = face_ref[parts, :, :surface]
             plain = wide_ref[...]
-            side_high_ref[...], side_low_ref[...] = split_pair(plain.T)
+            side_high_ref[:surface], side_low_ref[:surface] = split_pair(face_ref[parts, :, :surface].T)
+            side_high_ref[surface:] = jnp.zeros((corner, surface), jnp.bfloat16)
+            side_low_ref[surface:] = jnp.zeros((corner, surface), jnp.bfloat16)
             across_high_ref[...], across_low_ref[...] = split_pair(plain)
 
-    first = pl.multiple_of(jnp.where(slice_now == 0, 0, corner), 8)
-    face_full_ref[:, pl.ds(first, surface), :] = face_ref[:parts]
     side = (side_high_ref[...], side_low_ref[...])
     across = (across_high_ref[...], across_low_ref[...])
-    (through_real,) = product_stacked([side], split_pair(face_full_ref[0]))
-    (through_imag,) = product_stacked([side], split_pair(face_full_ref[1]))
+    (through_real,) = product_stacked([side], split_pair(face_ref[0]))
+    (through_imag,) = product_stacked([side], split_pair(face_ref[1]))
     term_real, term_imag = product_stacked([split_pair(through_real), split_pair(through_imag)], across)
     green = inverse_pair(known_ref[0] - term_real, known_ref[1] - term_imag)
     for piece, segments in enumerate(pieces):
@@ -194,35 +221,52 @@
 
 def scatter_kernel(
     energies_all, momenta_all, energies_here, momenta_here, momentum_groups, branches, slots,
-    offset_ref, strength_ref, coefficient_ref, mask_ref, in_ref, out_ref, mixed_ref,
+    group_ref, factor_ref, pattern_ref, in_ref, out_ref, mixed_ref,
 ):
+    table_size = momenta_all * momenta_all
+    offsets = [jnp.max(factor_ref[table_size + branches + branch]).astype(jnp.int32) for branch in range(branches)]
+
     def place(energy, momentum):
         group = (energy // energies_here) * momentum_groups + momentum // momenta_here
         return slots[group], (energy % energies_here) * momenta_here + momentum % momenta_here
 
+    piece_rows = in_ref.shape[2]
+    per_energy = pattern_ref.shape[1]
+    if piece_rows <= per_energy:
+        first = lax.rem(group_ref[0] * piece_rows, per_energy)
+        mask = pattern_ref[0, pl.ds(pl.multiple_of(first, piece_rows), piece_rows), :]
+    else:
+        mask = jnp.concatenate([pattern_ref[0]] * (piece_rows // per_energy), axis=0)
+    mask = mask.astype(jnp.float32)
     mixed_ref[energies_all] = jnp.zeros(mixed_ref.shape[1:], jnp.float32)
     for energy in range(energies_all):
         blocks = [in_ref[place(energy, momentum)] for momentum in range(momenta_all)]
         for target in range(momenta_all):
-            total = coefficient_ref[target, 0] * blocks[0]
+            total = factor_ref[target * momenta_all] * blocks[0]
             for momentum in range(1, momenta_all):
-                total = total + coefficient_ref[target, momentum] * blocks[momentum]
+                total = total + factor_ref[target * momenta_all + momentum] * blocks[momentum]
             mixed_ref[energy, target] = total
-    mask = mask_ref[...].astype(jnp.float32)
     for energy in range(energies_all):
         sources = []
         for branch in range(branches):
-            below = energy - offset_ref[branch]
-            above = energy + offset_ref[branch]
+            below = energy - offsets[branch]
+            above = energy + offsets[branch]
             below = jnp.where(jnp.logical_and(below >= 0, below < energies_all), below, energies_all)
             above = jnp.where(jnp.logical_and(above >= 0, above < energies_all), above, energies_all)
-            sources.append((strength_ref[branch], below, above))
+            sources.append((factor_ref[table_size + branch], below, above))
         for target in range(momenta_all):
             total = None
             for strength, below, above in sources:
                 term = strength * (mixed_ref[below, target] + mixed_ref[above, target])
                 total = term if total is None else total + term
             out_ref[place(energy, target)] = total * mask
+
+
+def momentum_coefficients(momentum_table, momentum_weights):
+    momentum_count = momentum_table.shape[0]
+    labels = jnp.arange(momentum_count, dtype=jnp.int32)
+    matches = momentum_table[:, :, None] == labels[None, None, :]
+    return jnp.sum(jnp.where(matches, momentum_weights[None, :, None], 0.0), axis=1)
 
 
 def assemble_kernel(pieces, in_ref, out_ref, semaphores):
@@ -259,13 +303,6 @@
                 start, left = start + count, left - count
             pieces.append(segments)
     return piece_rows, pieces
-
-
-def momentum_coefficients(momentum_table, momentum_weights):
-    momentum_count = momentum_table.shape[0]
-    labels = jnp.arange(momentum_count, dtype=jnp.int32)
-    matches = momentum_table[:, :, None] == labels[None, None, :]
-    return jnp.sum(jnp.where(matches, momentum_weights[None, :, None], 0.0), axis=1)
 
 
 def product_split(left_side, right_side):
@@ -330,7 +367,7 @@
 float_vmem = functools.partial(pltpu.VMEM, dtype=jnp.float32)
 
 
-def green_two_slices(hamiltonian, coupling, self_blocks, shift, position, pieces, blocks_shape):
+def green_two_slices(hamiltonian, coupling, self_blocks, shift, position, pieces, blocks_shape, small):
     orbitals, surface = hamiltonian.shape[-1], coupling.shape[-1]
     items = self_blocks.shape[0]
     slice_now = position.astype(jnp.int32).reshape(1)
@@ -344,31 +381,38 @@
     inverse_flops = 18 * orbitals**3
     swap = [(0, 1), (1, 0)]
 
+    shift = jnp.broadcast_to(shift[:, None, None], (items, 1, orbitals))
     self_blocks, base, term = (
         pltpu.with_memory_space_constraint(array, pltpu.HBM) for array in (self_blocks, hamiltonian, coupling)
     )
+    small = [pltpu.with_memory_space_constraint(array, pltpu.HBM) for array in small]
+    factor_count = small[0].size + small[2].size + small[3].size
     known, faces, sent = [], [], []
     later = []
     for item in range(items):
         first = item == 0
-        scratch = [float_vmem(pair)]
+        scratch = []
         if first:
             scratch += [float_vmem(pair), float_vmem(order), float_vmem((surface, surface)), float_vmem(order)]
-            scratch += [pltpu.SemaphoreType.DMA((2 + items * parts,))]
-        extra_shapes = [floats(order), floats(order)] + [floats(pair)] * (items - 1) if first else []
+            scratch += [pltpu.SMEM(array.shape, array.dtype) for array in small]
+            scratch += [pltpu.SemaphoreType.DMA((2 + items * parts,)), pltpu.SemaphoreType.DMA((len(small),))]
+        extra_shapes = []
+        if first:
+            extra_shapes = [floats(order), floats(order), floats((factor_count, 1, orbitals))]
+            extra_shapes += [floats(pair)] * (items - 1)
         result = pl.pallas_call(
             functools.partial(start_kernel, item, items, surface),
-            in_specs=[on_chip(), on_chip()] + [far if first else whole] * 3,
+            in_specs=[on_chip(), whole] + ([far] * (3 + len(small)) if first else [whole] * 3),
             out_specs=[whole] * (2 + len(extra_shapes)),
             out_shape=[floats(pair), floats((parts + first, surface, orbitals))] + extra_shapes,
             scratch_shapes=scratch,
             compiler_params=params,
             cost_estimate=pl.CostEstimate(flops=inverse_flops, bytes_accessed=0, transcendentals=0),
             name=f"start{item}",
-        )(slice_now, shift, base, term, self_blocks if first else later[item - 1])
+        )(slice_now, shift, base, term, *([self_blocks] + small if first else [later[item - 1]]))
         known.append(result[0])
         if first:
-            base, term, *later = result[2:]
+            base, term, factors, *later = result[2:]
         sent.append(result[1])
         faces.append(lax.ppermute(result[1], "space", swap))
 
@@ -381,8 +425,8 @@
             functools.partial(finish_kernel, item, items, surface, pieces),
             in_specs=[on_chip()] + [whole] * (len(operands) - 1),
             out_specs=[whole] * (5 if first else 1),
-            out_shape=out_shape + ([halves(order)] * 4 if first else []),
-            scratch_shapes=[float_vmem(pair)] + ([float_vmem(order)] if first else []),
+            out_shape=out_shape + ([halves((orbitals, surface))] * 2 + [halves(order)] * 2 if first else []),
+            scratch_shapes=[float_vmem(order)] if first else [],
             compiler_params=params,
             cost_estimate=pl.CostEstimate(flops=2 * inverse_flops, bytes_accessed=0, transcendentals=0),
             name=f"finish{item}",
@@ -390,7 +434,7 @@
         greens.append(result[0])
         if first:
             sides = list(result[1:])
-    return greens[-1]
+    return greens[-1], factors
 
 
 def body(
@@ -427,11 +471,17 @@
     pieces = [pieces[member] for member in members]
     blocks_shape = (len(pieces), items, piece_rows, orbitals)
     if lax.axis_size("space") == 2:
-        green = green_two_slices(hamiltonian, coupling, self_blocks, shift, position, pieces, blocks_shape)
+        small = (momentum_table, momentum_weights, mode_strengths, mode_offsets)
+        green, factors = green_two_slices(
+            hamiltonian, coupling, self_blocks, shift, position, pieces, blocks_shape, small
+        )
     else:
         slices = lax.axis_size("space")
         green = green_by_sweeps(hamiltonian[0], coupling[0], self_blocks, shift, position, slices)
         green = cut_pieces(green, pieces)
+        factors = momentum_coefficients(momentum_table, momentum_weights).reshape(-1)
+        factors = jnp.concatenate([factors, mode_strengths, mode_offsets.astype(jnp.float32)])
+        factors = jnp.broadcast_to(factors[:, None, None], (factors.shape[0], 1, orbitals))
 
     exchange = functools.partial(
         lax.all_to_all,
@@ -441,23 +491,18 @@
         axis_index_groups=[members],
         tiled=True,
     )
-    coefficients = momentum_coefficients(momentum_table, momentum_weights)
-    mask_rows = jnp.concatenate([pattern[0]] * parts, axis=0)
-    mask_rows = lax.dynamic_slice_in_dim(mask_rows, lax.axis_index("mom") * piece_rows, piece_rows, 0)
-    green, coefficients, mask_rows, mode_offsets, mode_strengths = lax.optimization_barrier(
-        (green, coefficients, mask_rows, mode_offsets, mode_strengths)
-    )
+    momentum_group = lax.axis_index("mom").astype(jnp.int32).reshape(1)
     gathered = exchange(green)
     scattered = pl.pallas_call(
         functools.partial(
             scatter_kernel, energies_all, momenta_all, energies_here, momenta_here, momentum_groups, branches, slots
         ),
-        in_specs=[on_chip(), on_chip(), on_chip(), pl.BlockSpec(), pl.BlockSpec()],
+        in_specs=[on_chip()] + [pl.BlockSpec(memory_space=pltpu.VMEM)] * 3,
         out_shape=jax.ShapeDtypeStruct(blocks_shape, jnp.float32),
         scratch_shapes=[float_vmem((energies_all + 1, momenta_all, piece_rows, orbitals))],
         compiler_params=pltpu.CompilerParams(vmem_limit_bytes=kernel_memory),
         name="scatter",
-    )(mode_offsets, mode_strengths, coefficients, mask_rows, gathered)
+    )(momentum_group, factors, pattern, gathered)
     returned = exchange(scattered)
     copies = items * sum(len(segments) for segments in pieces)
     whole = pl.pallas_call(

time: 72.7 us -> 71.5 us (0.983)
  Pallas kernels: 9.8 us -> 8.05 us
  waiting for transfers between devices: 0.01 us -> 0.96 us
    pallas_call x2, Pallas kernels: 3.94 us -> 2.88 us  [green_two_slices(): pl.pallas_call(functools.partial(start_kernel, item, items, surface), in_...]
    ppermute x2, waiting for transfers between devices: 0.01 us -> 0.96 us  [green_two_slices(): faces.append(lax.ppermute(result[1], 'space', swap))]
  transfers between devices with their start and end apart: 2 -> 2, of which waited for: 0 -> 1; matrix products, arithmetic and copies ran while one was open for 0% -> 0% of each run, Pallas kernels for 4% -> 4%
where the time goes in v4:
time: 71.5 us; the launch traced here: 71.2 us
  blocking collectives  61.1 us (85%)
  Pallas kernels  8.05 us (11%)
  waiting for transfers between devices  0.96 us (1%)
  starting transfers between devices  0.92 us (1%)
    all_to_all x1, blocking collectives, body(): gathered = exchange(green)  33 us
    all_to_all x1, blocking collectives, body(): returned = exchange(scattered)  28.2 us
    pallas_call x2, Pallas kernels, green_two_slices(): pl.pallas_call(functools.partial(finish_kernel, item, items, surface, pie...  3.42 us
    pallas_call x2, Pallas kernels, green_two_slices(): pl.pallas_call(functools.partial(start_kernel, item, items, surface), in_...  2.88 us
  transfers between devices with their start and end apart: 2, of which 1 were waited for; matrix products, arithmetic and copies ran while one was open for 0% of the time, Pallas kernels for 4%

profile of v4, /device:TPU:0, one launch (start us, length us, event | category | flops | bytes accessed | tf_op | source)
XLA Modules:
  0.0 71.2 jit_solution(12062437856780033525)
XLA Ops:
  0.0 0.1 broadcast_in_dim.2.shift_ref
  0.1 2.2 %start0.1 = (f32[2,256,256]{2,1,0:T(8,128)S(1)}, f32[3,224,256]{2,1,0:T(8,128)S(1)}, f32[256,256]{1,0:T(8,128)S(1)}, f32[256,256]{1,0:T(8,128)S(1)}, f32[20,1,25...) custom-call(s32[1]{0:T(128)} %bitcast.1.slice_ref.refs_0_, f32[2,1,256]{2,1,0:T(1,128)S(1)} %broadcast_in_dim.2.shift_ref, ...), custom_call_target="tpu_custom_call" | custom-call | flops 301989888 | tf_op jit(solution)/shard_map/start0/pallas_call | solution.py:403
  2.3 0.8 %collective-permute-start.1 = (f32[3,224,256]{2,1,0:T(8,128)S(1)}, f32[3,224,256]{2,1,0:T(8,128)S(1)}, u32[]{:S(2)}, u32[]{:S(2)}) collective-permute-start(f32[3,224,256]{2,1,0:T(8,128)S(1)} %get-tuple-element.25.refs_3_), channel_id=1, source_target_pairs={{0,16},{16,0},{1,17},{17,1},{2,18},{18,2},{3,19},{19,3},{4,20},{20... | collective-permute-start | bytes 2064392 | tf_op jit(solution)/shard_map/ppermute | solution.py:417
  3.1 0.7 %start1.1 = (f32[2,256,256]{2,1,0:T(8,128)S(1)}, f32[2,224,256]{2,1,0:T(8,128)S(1)}) custom-call(s32[1]{0:T(128)} %bitcast.1.slice_ref.refs_0_, f32[2,1,256]{2,1,0:T(1,128)S(1)} %broadcast_in_dim.2.shift_ref, f32[256,256]{1,0:T(8,128)S(1)} %get-tuple-element.19.base_from_ref, f32[256,256]{1,0:T(8,128)S(1)} %get-tuple-element.20.term_from_ref, ...), custom_call_target="tpu_custom_call" | custom-call | flops 301989888 | tf_op jit(solution)/shard_map/start1/pallas_call | solution.py:403
  3.8 0.1 collective-permute-start
  3.9 1.0 %collective-permute-done.1.refs_2_ = f32[3,224,256]{2,1,0:T(8,128)S(1)} collective-permute-done((f32[3,224,256]{2,1,0:T(8,128)S(1)}, f32[3,224,256]{2,1,0:T(8,128)S(1)}, u32[]{:S(2)}, u32[]{:S(2)}) %collective-permute-start.1) | collective-permute-done | bytes 688160 | tf_op jit(solution)/shard_map/ppermute | solution.py:417
  4.9 1.8 %finish0.1 = (f32[16,32,256]{2,1,0:T(8,128)S(1)}, bf16[256,224]{1,0:T(8,128)(2,1)S(1)}, bf16[256,224]{1,0:T(8,128)(2,1)S(1)}, bf16[256,256]{1,0:T(8,128)(2,1)S(1)}, bf16[256,256]{1,0:T(8,128)(2,1)S(1)}) custom-call(s32[1]{0:T(128)} %bitcast.1.slice_ref.refs_0_, f32[2,256,256]{2,1,0:T(8,128)S(1)} %get-tuple-element.24.refs_1_, ...), custom_call_target="tpu_custom_call" | custom-call | flops 603979776 | tf_op jit(solution)/shard_map/finish0/pallas_call | solution.py:424
  6.7 0.0 collective-permute-done.refs_2_
  6.7 1.6 %finish1.1 = f32[16,2,32,256]{3,2,1,0:T(8,128)S(1)} custom-call(s32[1]{0:T(128)} %bitcast.1.slice_ref.refs_0_, f32[2,256,256]{2,1,0:T(8,128)S(1)} %get-tuple-element.22.refs_1_, f32[2,224,256]{2,1,0:T(8,128)S(1)} %collective-permute-done.refs_2_, bf16[256,224]{1,0:T(8,128)(2,1)S(1)} %get-tuple-element.26.refs_3_, ...), custom_call_target="tpu_custom_call" | custom-call | flops 603979776 | tf_op jit(solution)/shard_map/finish1/pallas_call | solution.py:424
  8.3 0.0 copy-start
  8.3 33.0 %all_to_all.10.in_ref = f32[16,2,32,256]{3,2,1,0:T(8,128)S(1)} all-to-all(f32[16,2,32,256]{3,2,1,0:T(8,128)S(1)} %finish1.1), channel_id=1, replica_groups={{6,8,4,11,2,13,10,9,5,12,3,7,1,15,0,14},{22,24,20,27,18,29,26,25,21,28,..., dimensions={0} | all-to-all | bytes 2097152 | tf_op jit(solution)/shard_map/all_to_all | solution.py:495
  41.3 0.0 copy-done
  41.3 0.5 scatter.1
  41.9 28.2 %all_to_all.11.in_ref = f32[16,2,32,256]{3,2,1,0:T(8,128)S(1)} all-to-all(f32[16,2,32,256]{3,2,1,0:T(8,128)S(1)} %scatter.1), channel_id=1, replica_groups={{6,8,4,11,2,13,10,9,5,12,3,7,1,15,0,14},{22,24,20,27,18,29,26,25,21,28,..., dimensions={0} | all-to-all | bytes 2097152 | tf_op jit(solution)/shard_map/all_to_all | solution.py:506
  70.0 1.2 %assemble.1 = f32[2,2,256,256]{3,2,1,0:T(8,128)} custom-call(f32[16,2,32,256]{3,2,1,0:T(8,128)S(1)} %all_to_all.11.in_ref), custom_call_target="tpu_custom_call" | custom-call | tf_op jit(solution)/shard_map/assemble/pallas_call | solution.py:508
  (1 shorter events, 0.0 us)
Async XLA Ops:
  2.3 2.6 %collective-permute-start.1 = (f32[3,224,256]{2,1,0:T(8,128)S(1)}, f32[3,224,256]{2,1,0:T(8,128)S(1)}, u32[]{:S(2)}, u32[]{:S(2)}) collective-permute-start(f32[3,224,256]{2,1,0:T(8,128)S(1)} %get-tuple-element.25.refs_3_), channel_id=1, source_target_pairs={{0,16},{16,0},{1,17},{17,1},{2,18},{18,2},{3,19},{19,3},{4,20},{20... | collective-permute-start | bytes 2064392 | tf_op jit(solution)/shard_map/ppermute | solution.py:417
  3.8 2.8 %collective-permute-start = (f32[2,224,256]{2,1,0:T(8,128)S(1)}, f32[2,224,256]{2,1,0:T(8,128)S(1)}, u32[]{:S(2)}, u32[]{:S(2)}) collective-permute-start(f32[2,224,256]{2,1,0:T(8,128)S(1)} %get-tuple-element.23), channel_id=1, source_target_pairs={{0,16},{16,0},{1,17},{17,1},{2,18},{18,2},{3,19},{19,3},{4,20},{20... | collective-permute-start | bytes 1376264 | tf_op jit(solution)/shard_map/ppermute | solution.py:417
  8.3 33.0 %copy-start = (s32[1,32,256]{2,1,0:T(8,128)S(1)}, s32[1,32,256]{2,1,0:T(8,128)}, u32[]{:S(2)}) copy-start(s32[1,32,256]{2,1,0:T(8,128)} %pattern_ref.1) | copy-start | bytes 98308

commit v5 on v4

--- a/solution.py
+++ b/solution.py
@@ -13,7 +13,7 @@
 dispersion = 1.0
 parts = 2
 kernel_memory = 24 * 1024 * 1024
-member_seed = 117
+member_seed = 79
 
 
 def split_pair(value):

time: 71.5 us -> 69.2 us (0.968)
  blocking collectives: 61.1 us -> 58.8 us
    all_to_all x1, blocking collectives: 33 us -> 30.2 us  [body(): gathered = exchange(green)]
where the time goes in v5:
time: 69.2 us; the launch traced here: 68.9 us
  blocking collectives  58.8 us (85%)
  Pallas kernels  8.05 us (12%)
  waiting for transfers between devices  0.96 us (1%)
  starting transfers between devices  0.92 us (1%)
    all_to_all x1, blocking collectives, body(): gathered = exchange(green)  30.2 us
    all_to_all x1, blocking collectives, body(): returned = exchange(scattered)  28.6 us
    pallas_call x2, Pallas kernels, green_two_slices(): pl.pallas_call(functools.partial(finish_kernel, item, items, surface, pie...  3.42 us
    pallas_call x2, Pallas kernels, green_two_slices(): pl.pallas_call(functools.partial(start_kernel, item, items, surface), in_...  2.88 us
  transfers between devices with their start and end apart: 2, of which 1 were waited for; matrix products, arithmetic and copies ran while one was open for 0% of the time, Pallas kernels for 4%

profile of v5, /device:TPU:0, one launch (start us, length us, event | category | flops | bytes accessed | tf_op | source)
XLA Modules:
  0.0 68.9 jit_solution(14871484082973073841)
XLA Ops:
  0.0 0.1 broadcast_in_dim.2.shift_ref
  0.1 2.2 %start0.1 = (f32[2,256,256]{2,1,0:T(8,128)S(1)}, f32[3,224,256]{2,1,0:T(8,128)S(1)}, f32[256,256]{1,0:T(8,128)S(1)}, f32[256,256]{1,0:T(8,128)S(1)}, f32[20,1,25...) custom-call(s32[1]{0:T(128)} %bitcast.1.slice_ref.refs_0_, f32[2,1,256]{2,1,0:T(1,128)S(1)} %broadcast_in_dim.2.shift_ref, ...), custom_call_target="tpu_custom_call" | custom-call | flops 301989888 | tf_op jit(solution)/shard_map/start0/pallas_call | solution.py:403
  2.3 0.8 %collective-permute-start.1 = (f32[3,224,256]{2,1,0:T(8,128)S(1)}, f32[3,224,256]{2,1,0:T(8,128)S(1)}, u32[]{:S(2)}, u32[]{:S(2)}) collective-permute-start(f32[3,224,256]{2,1,0:T(8,128)S(1)} %get-tuple-element.25.refs_3_), channel_id=1, source_target_pairs={{0,16},{16,0},{1,17},{17,1},{2,18},{18,2},{3,19},{19,3},{4,20},{20... | collective-permute-start | bytes 2064392 | tf_op jit(solution)/shard_map/ppermute | solution.py:417
  3.1 0.7 %start1.1 = (f32[2,256,256]{2,1,0:T(8,128)S(1)}, f32[2,224,256]{2,1,0:T(8,128)S(1)}) custom-call(s32[1]{0:T(128)} %bitcast.1.slice_ref.refs_0_, f32[2,1,256]{2,1,0:T(1,128)S(1)} %broadcast_in_dim.2.shift_ref, f32[256,256]{1,0:T(8,128)S(1)} %get-tuple-element.19.base_from_ref, f32[256,256]{1,0:T(8,128)S(1)} %get-tuple-element.20.term_from_ref, ...), custom_call_target="tpu_custom_call" | custom-call | flops 301989888 | tf_op jit(solution)/shard_map/start1/pallas_call | solution.py:403
  3.8 0.1 collective-permute-start
  3.9 1.0 %collective-permute-done.1.refs_2_ = f32[3,224,256]{2,1,0:T(8,128)S(1)} collective-permute-done((f32[3,224,256]{2,1,0:T(8,128)S(1)}, f32[3,224,256]{2,1,0:T(8,128)S(1)}, u32[]{:S(2)}, u32[]{:S(2)}) %collective-permute-start.1) | collective-permute-done | bytes 688160 | tf_op jit(solution)/shard_map/ppermute | solution.py:417
  4.9 1.8 %finish0.1 = (f32[16,32,256]{2,1,0:T(8,128)S(1)}, bf16[256,224]{1,0:T(8,128)(2,1)S(1)}, bf16[256,224]{1,0:T(8,128)(2,1)S(1)}, bf16[256,256]{1,0:T(8,128)(2,1)S(1)}, bf16[256,256]{1,0:T(8,128)(2,1)S(1)}) custom-call(s32[1]{0:T(128)} %bitcast.1.slice_ref.refs_0_, f32[2,256,256]{2,1,0:T(8,128)S(1)} %get-tuple-element.24.refs_1_, ...), custom_call_target="tpu_custom_call" | custom-call | flops 603979776 | tf_op jit(solution)/shard_map/finish0/pallas_call | solution.py:424
  6.7 0.0 collective-permute-done.refs_2_
  6.7 1.6 %finish1.1 = f32[16,2,32,256]{3,2,1,0:T(8,128)S(1)} custom-call(s32[1]{0:T(128)} %bitcast.1.slice_ref.refs_0_, f32[2,256,256]{2,1,0:T(8,128)S(1)} %get-tuple-element.22.refs_1_, f32[2,224,256]{2,1,0:T(8,128)S(1)} %collective-permute-done.refs_2_, bf16[256,224]{1,0:T(8,128)(2,1)S(1)} %get-tuple-element.26.refs_3_, ...), custom_call_target="tpu_custom_call" | custom-call | flops 603979776 | tf_op jit(solution)/shard_map/finish1/pallas_call | solution.py:424
  8.3 0.0 copy-start
  8.3 30.2 %all_to_all.10.in_ref = f32[16,2,32,256]{3,2,1,0:T(8,128)S(1)} all-to-all(f32[16,2,32,256]{3,2,1,0:T(8,128)S(1)} %finish1.1), channel_id=1, replica_groups={{11,0,6,5,12,9,15,1,14,2,8,4,3,10,13,7},{27,16,22,21,28,25,31,17,30,18,..., dimensions={0} | all-to-all | bytes 2097152 | tf_op jit(solution)/shard_map/all_to_all | solution.py:495
  38.5 0.0 copy-done
  38.5 0.5 scatter.1
  39.1 28.6 %all_to_all.11.in_ref = f32[16,2,32,256]{3,2,1,0:T(8,128)S(1)} all-to-all(f32[16,2,32,256]{3,2,1,0:T(8,128)S(1)} %scatter.1), channel_id=1, replica_groups={{11,0,6,5,12,9,15,1,14,2,8,4,3,10,13,7},{27,16,22,21,28,25,31,17,30,18,..., dimensions={0} | all-to-all | bytes 2097152 | tf_op jit(solution)/shard_map/all_to_all | solution.py:506
  67.7 1.2 %assemble.1 = f32[2,2,256,256]{3,2,1,0:T(8,128)} custom-call(f32[16,2,32,256]{3,2,1,0:T(8,128)S(1)} %all_to_all.11.in_ref), custom_call_target="tpu_custom_call" | custom-call | tf_op jit(solution)/shard_map/assemble/pallas_call | solution.py:508
  (1 shorter events, 0.0 us)
Async XLA Ops:
  2.3 2.6 %collective-permute-start.1 = (f32[3,224,256]{2,1,0:T(8,128)S(1)}, f32[3,224,256]{2,1,0:T(8,128)S(1)}, u32[]{:S(2)}, u32[]{:S(2)}) collective-permute-start(f32[3,224,256]{2,1,0:T(8,128)S(1)} %get-tuple-element.25.refs_3_), channel_id=1, source_target_pairs={{0,16},{16,0},{1,17},{17,1},{2,18},{18,2},{3,19},{19,3},{4,20},{20... | collective-permute-start | bytes 2064392 | tf_op jit(solution)/shard_map/ppermute | solution.py:417
  3.8 2.8 %collective-permute-start = (f32[2,224,256]{2,1,0:T(8,128)S(1)}, f32[2,224,256]{2,1,0:T(8,128)S(1)}, u32[]{:S(2)}, u32[]{:S(2)}) collective-permute-start(f32[2,224,256]{2,1,0:T(8,128)S(1)} %get-tuple-element.23), channel_id=1, source_target_pairs={{0,16},{16,0},{1,17},{17,1},{2,18},{18,2},{3,19},{19,3},{4,20},{20... | collective-permute-start | bytes 1376264 | tf_op jit(solution)/shard_map/ppermute | solution.py:417
  8.3 30.2 %copy-start = (s32[1,32,256]{2,1,0:T(8,128)S(1)}, s32[1,32,256]{2,1,0:T(8,128)}, u32[]{:S(2)}) copy-start(s32[1,32,256]{2,1,0:T(8,128)} %pattern_ref.1) | copy-start | bytes 98308

commit v6 on v5

--- a/solution.py
+++ b/solution.py
@@ -114,7 +114,7 @@
                 self_copies.append(copy)
         coupling_copy = pltpu.make_async_copy(term_from_ref.at[0], coupling_buffer, semaphores.at[0])
         base_copy = pltpu.make_async_copy(base_from_ref.at[0], base_buffer, semaphores.at[1])
-        for copy in [coupling_copy, base_copy] + self_copies[:parts] + small_copies + self_copies[parts:]:
+        for copy in small_copies + [coupling_copy, base_copy] + self_copies:
             copy.start()
     else:
         self_ref, known_ref, face_ref = rest
@@ -142,6 +142,9 @@
 
         base_copy.wait()
         base_ref[...] = 0.5 * (base_buffer[...] + base_buffer[...].T)
+        for copy in small_copies:
+            copy.wait()
+        write_factors(factor_ref, *near_refs)
         for copy in self_copies[:parts]:
             copy.wait()
     real_part = jnp.where(on_diagonal, shift_ref[item], 0.0) - base_ref[...] - self_ref[0]
@@ -161,9 +164,8 @@
         face_ref[1] = green_imag[:surface]
 
     if item == 0:
-        for copy in small_copies + self_copies[parts:]:
+        for copy in self_copies[parts:]:
             copy.wait()
-        write_factors(factor_ref, *near_refs)
 
 
 def finish_kernel(item, items, surface, pieces, *refs):

time: 69.2 us -> 69.1 us (level)
  no operation moved by 1% of the time
where the time goes in v6:
time: 69.1 us; the launch traced here: 68.9 us
  blocking collectives  58.8 us (85%)
  Pallas kernels  8.03 us (12%)
  waiting for transfers between devices  0.95 us (1%)
  starting transfers between devices  0.94 us (1%)
    all_to_all x1, blocking collectives, body(): gathered = exchange(green)  30.2 us
    all_to_all x1, blocking collectives, body(): returned = exchange(scattered)  28.6 us
    pallas_call x2, Pallas kernels, green_two_slices(): pl.pallas_call(functools.partial(finish_kernel, item, items, surface, pie...  3.41 us
    pallas_call x2, Pallas kernels, green_two_slices(): pl.pallas_call(functools.partial(start_kernel, item, items, surface), in_...  2.86 us
  transfers between devices with their start and end apart: 2, of which 1 were waited for; matrix products, arithmetic and copies ran while one was open for 0% of the time, Pallas kernels for 4%

profile of v6, /device:TPU:0, one launch (start us, length us, event | category | flops | bytes accessed | tf_op | source)
XLA Modules:
  0.0 68.9 jit_solution(12431353091666358876)
XLA Ops:
  0.0 0.1 broadcast_in_dim.2.shift_ref
  0.1 2.1 %start0.1 = (f32[2,256,256]{2,1,0:T(8,128)S(1)}, f32[3,224,256]{2,1,0:T(8,128)S(1)}, f32[256,256]{1,0:T(8,128)S(1)}, f32[256,256]{1,0:T(8,128)S(1)}, f32[20,1,25...) custom-call(s32[1]{0:T(128)} %bitcast.1.slice_ref.refs_0_, f32[2,1,256]{2,1,0:T(1,128)S(1)} %broadcast_in_dim.2.shift_ref, ...), custom_call_target="tpu_custom_call" | custom-call | flops 301989888 | tf_op jit(solution)/shard_map/start0/pallas_call | solution.py:405
  2.3 0.8 %collective-permute-start.1 = (f32[3,224,256]{2,1,0:T(8,128)S(1)}, f32[3,224,256]{2,1,0:T(8,128)S(1)}, u32[]{:S(2)}, u32[]{:S(2)}) collective-permute-start(f32[3,224,256]{2,1,0:T(8,128)S(1)} %get-tuple-element.25.refs_3_), channel_id=1, source_target_pairs={{0,16},{16,0},{1,17},{17,1},{2,18},{18,2},{3,19},{19,3},{4,20},{20... | collective-permute-start | bytes 2064392 | tf_op jit(solution)/shard_map/ppermute | solution.py:419
  3.1 0.7 %start1.1 = (f32[2,256,256]{2,1,0:T(8,128)S(1)}, f32[2,224,256]{2,1,0:T(8,128)S(1)}) custom-call(s32[1]{0:T(128)} %bitcast.1.slice_ref.refs_0_, f32[2,1,256]{2,1,0:T(1,128)S(1)} %broadcast_in_dim.2.shift_ref, f32[256,256]{1,0:T(8,128)S(1)} %get-tuple-element.19.base_from_ref, f32[256,256]{1,0:T(8,128)S(1)} %get-tuple-element.20.term_from_ref, ...), custom_call_target="tpu_custom_call" | custom-call | flops 301989888 | tf_op jit(solution)/shard_map/start1/pallas_call | solution.py:405
  3.8 0.1 collective-permute-start
  3.9 0.9 %collective-permute-done.1.refs_2_ = f32[3,224,256]{2,1,0:T(8,128)S(1)} collective-permute-done((f32[3,224,256]{2,1,0:T(8,128)S(1)}, f32[3,224,256]{2,1,0:T(8,128)S(1)}, u32[]{:S(2)}, u32[]{:S(2)}) %collective-permute-start.1) | collective-permute-done | bytes 688160 | tf_op jit(solution)/shard_map/ppermute | solution.py:419
  4.9 1.8 %finish0.1 = (f32[16,32,256]{2,1,0:T(8,128)S(1)}, bf16[256,224]{1,0:T(8,128)(2,1)S(1)}, bf16[256,224]{1,0:T(8,128)(2,1)S(1)}, bf16[256,256]{1,0:T(8,128)(2,1)S(1)}, bf16[256,256]{1,0:T(8,128)(2,1)S(1)}) custom-call(s32[1]{0:T(128)} %bitcast.1.slice_ref.refs_0_, f32[2,256,256]{2,1,0:T(8,128)S(1)} %get-tuple-element.24.refs_1_, ...), custom_call_target="tpu_custom_call" | custom-call | flops 603979776 | tf_op jit(solution)/shard_map/finish0/pallas_call | solution.py:426
  6.7 0.0 collective-permute-done.refs_2_
  6.7 1.6 %finish1.1 = f32[16,2,32,256]{3,2,1,0:T(8,128)S(1)} custom-call(s32[1]{0:T(128)} %bitcast.1.slice_ref.refs_0_, f32[2,256,256]{2,1,0:T(8,128)S(1)} %get-tuple-element.22.refs_1_, f32[2,224,256]{2,1,0:T(8,128)S(1)} %collective-permute-done.refs_2_, bf16[256,224]{1,0:T(8,128)(2,1)S(1)} %get-tuple-element.26.refs_3_, ...), custom_call_target="tpu_custom_call" | custom-call | flops 603979776 | tf_op jit(solution)/shard_map/finish1/pallas_call | solution.py:426
  8.3 0.0 copy-start
  8.3 30.2 %all_to_all.10.in_ref = f32[16,2,32,256]{3,2,1,0:T(8,128)S(1)} all-to-all(f32[16,2,32,256]{3,2,1,0:T(8,128)S(1)} %finish1.1), channel_id=1, replica_groups={{11,0,6,5,12,9,15,1,14,2,8,4,3,10,13,7},{27,16,22,21,28,25,31,17,30,18,..., dimensions={0} | all-to-all | bytes 2097152 | tf_op jit(solution)/shard_map/all_to_all | solution.py:497
  38.5 0.0 copy-done
  38.5 0.5 scatter.1
  39.0 28.6 %all_to_all.11.in_ref = f32[16,2,32,256]{3,2,1,0:T(8,128)S(1)} all-to-all(f32[16,2,32,256]{3,2,1,0:T(8,128)S(1)} %scatter.1), channel_id=1, replica_groups={{11,0,6,5,12,9,15,1,14,2,8,4,3,10,13,7},{27,16,22,21,28,25,31,17,30,18,..., dimensions={0} | all-to-all | bytes 2097152 | tf_op jit(solution)/shard_map/all_to_all | solution.py:508
  67.6 1.2 %assemble.1 = f32[2,2,256,256]{3,2,1,0:T(8,128)} custom-call(f32[16,2,32,256]{3,2,1,0:T(8,128)S(1)} %all_to_all.11.in_ref), custom_call_target="tpu_custom_call" | custom-call | tf_op jit(solution)/shard_map/assemble/pallas_call | solution.py:510
  (1 shorter events, 0.0 us)
Async XLA Ops:
  2.3 2.6 %collective-permute-start.1 = (f32[3,224,256]{2,1,0:T(8,128)S(1)}, f32[3,224,256]{2,1,0:T(8,128)S(1)}, u32[]{:S(2)}, u32[]{:S(2)}) collective-permute-start(f32[3,224,256]{2,1,0:T(8,128)S(1)} %get-tuple-element.25.refs_3_), channel_id=1, source_target_pairs={{0,16},{16,0},{1,17},{17,1},{2,18},{18,2},{3,19},{19,3},{4,20},{20... | collective-permute-start | bytes 2064392 | tf_op jit(solution)/shard_map/ppermute | solution.py:419
  3.8 2.8 %collective-permute-start = (f32[2,224,256]{2,1,0:T(8,128)S(1)}, f32[2,224,256]{2,1,0:T(8,128)S(1)}, u32[]{:S(2)}, u32[]{:S(2)}) collective-permute-start(f32[2,224,256]{2,1,0:T(8,128)S(1)} %get-tuple-element.23), channel_id=1, source_target_pairs={{0,16},{16,0},{1,17},{17,1},{2,18},{18,2},{3,19},{19,3},{4,20},{20... | collective-permute-start | bytes 1376264 | tf_op jit(solution)/shard_map/ppermute | solution.py:419
  8.3 30.2 %copy-start = (s32[1,32,256]{2,1,0:T(8,128)S(1)}, s32[1,32,256]{2,1,0:T(8,128)}, u32[]{:S(2)}) copy-start(s32[1,32,256]{2,1,0:T(8,128)} %pattern_ref.1) | copy-start | bytes 98308
